TPU v7x, 32 devices: a whole 2x2x4 slice. The times are simulated.
32 devices in a mesh: ep: 16 (over z, y, core), dp: 2 (over x).
Axes of the slice: x: 2, y: 2, z: 4, core: 2. Of those that a mesh axis runs over, the one named last changes fastest.
Arguments:
- hidden: bfloat16 [2, 1024, 2048], P(None, ('ep', 'dp')), may hold values from -6 to 6
- norm_gain: bfloat16 [2048], replicated, may hold values from 0.5 to 1.5
- gate_weights: float32 [2, 1024, 8], P(None, ('ep', 'dp')), may hold values from 0.05 to 1
- routes: int32 [2, 1024, 8], P(None, ('ep', 'dp')), may hold values from 0 to 15, as said below
- replica_pick: int32 [2, 1024, 8], P(None, ('ep', 'dp')), may hold values from 0 to 1023
- trainer_experts: int32 [16], replicated, may hold values from 0 to 15, each once
- hot_experts: int32 [3], replicated, may hold values from 0 to 15, as said below
- replica_hot: int32 [16], replicated, may hold values from 0 to 2, as said below
- w_gate: bfloat16 [16, 2048, 384], P('ep', 'dp'), may hold values from -0.125 to 0.125
- w_up: bfloat16 [16, 2048, 384], P('ep', 'dp'), may hold values from -0.125 to 0.125
- w_down: bfloat16 [16, 384, 2048], P('ep', None, 'dp'), may hold values from -0.3125 to 0.3125
- queries: bfloat16 [2, 1024, 4096], P(None, ('ep', 'dp')), may hold values from -6 to 6
- key_cache: bfloat16 [1024, 32, 512], P(('ep', 'dp')), may hold values from -6 to 6
- value_cache: bfloat16 [1024, 32, 512], P(('ep', 'dp')), may hold values from -6 to 6
- new_keys: bfloat16 [2, 1024, 512], P(None, ('ep', 'dp')), may hold values from -6 to 6
- new_values: bfloat16 [2, 1024, 512], P(None, ('ep', 'dp')), may hold values from -6 to 6
- cache_lengths: int32 [1024], P(('ep', 'dp')), may hold values from 2 to 32, as said below
Outputs:
- mixed: bfloat16 [2, 1024, 2048], P(None, ('ep', 'dp'))
- context: bfloat16 [2, 1024, 4096], P(None, ('ep', 'dp'))
Inputs may be any that keep to these rules, and one draw needn't show every extreme that they name: Trainer index p holds expert trainer_experts[p]; each expert once. `hot_experts`: 3 different experts, among them expert 0 and expert 16 - 1. `replica_hot`: every entry of hot_experts is named by some index. `cache_lengths`: the 32 sequences of each device include one with 32 live entries. `routes`: each row names 8 different experts; every expert is named by some row.
All inputs are finite; a program needn't handle non-finite values.
Results may differ from a plain program's by a relative error of at most 0.001.
The roundings to bfloat16 on the way count: a program that leaves them out, or rounds other values in their place, can miss the bound.
Values may be sent and summed in bfloat16 or wider, within the bound.
No kernel may reach another device: no remote copies, remote signals or barrier semaphores. Data moves between devices by JAX's collectives and lax.ppermute only.
A program may use at most 64 MiB of HBM per device.

v0:
```python
import math

import jax
import jax.numpy as jnp
from jax import lax
from jax.sharding import PartitionSpec as P

HEADS = 32
KV_HEADS = 4
HEAD = 128
TOP = 8
CAP = 3
SLOTS = 2


norm_epsilon = 1e-06


def spread(shard, axis, root):
    mine = lax.axis_index(axis) == root
    return lax.psum(jnp.where(mine, shard, jnp.zeros_like(shard)), axis)


def scaled_norm(hidden_rows, norm_gain):
    values = hidden_rows.astype(jnp.float32)
    mean_square = jnp.mean(values * values, axis=-1, keepdims=True)
    return (values * lax.rsqrt(mean_square + norm_epsilon) * norm_gain.astype(jnp.float32)).astype(
        jnp.bfloat16
    )


def table_lookup(onehot_rows, table):
    return jnp.dot(onehot_rows, table, preferred_element_type=jnp.int32)


def attend(query_rows, key_cache, value_cache, new_keys, new_values, cache_lengths, step_index):
    rows_here = query_rows.shape[0]
    cache_len = key_cache.shape[1]
    steps_all = new_keys.shape[0]
    grouped = query_rows.reshape(rows_here, KV_HEADS, HEADS // KV_HEADS, HEAD)
    keys_cached = key_cache.reshape(rows_here, cache_len, KV_HEADS, HEAD)
    values_cached = value_cache.reshape(rows_here, cache_len, KV_HEADS, HEAD)
    keys_fresh = new_keys.reshape(steps_all, rows_here, KV_HEADS, HEAD)
    values_fresh = new_values.reshape(steps_all, rows_here, KV_HEADS, HEAD)
    score_scale = 1.0 / math.sqrt(HEAD)
    cache_scores = (
        jnp.einsum("rkgh,rckh->rkgc", grouped, keys_cached, preferred_element_type=jnp.float32)
        * score_scale
    )
    fresh_scores = (
        jnp.einsum("rkgh,srkh->rkgs", grouped, keys_fresh, preferred_element_type=jnp.float32)
        * score_scale
    )
    cache_mask = (jnp.arange(cache_len, dtype=jnp.int32)[None, :] < cache_lengths[:, None])[
        :, None, None, :
    ]
    fresh_mask = (jnp.arange(steps_all, dtype=jnp.int32) <= step_index)[None, None, None, :]
    row_max = jnp.maximum(
        jnp.max(jnp.where(cache_mask, cache_scores, -1e30), axis=-1),
        jnp.max(jnp.where(fresh_mask, fresh_scores, -1e30), axis=-1),
    )
    cache_exp = jnp.where(cache_mask, jnp.exp(cache_scores - row_max[..., None]), 0.0)
    fresh_exp = jnp.where(fresh_mask, jnp.exp(fresh_scores - row_max[..., None]), 0.0)
    row_total = jnp.sum(cache_exp, axis=-1) + jnp.sum(fresh_exp, axis=-1)
    cache_probs = (cache_exp / row_total[..., None]).astype(jnp.bfloat16)
    fresh_probs = (fresh_exp / row_total[..., None]).astype(jnp.bfloat16)
    summed = jnp.einsum(
        "rkgc,rckh->rkgh", cache_probs, values_cached, preferred_element_type=jnp.float32
    )
    summed = summed + jnp.einsum(
        "rkgs,srkh->rkgh", fresh_probs, values_fresh, preferred_element_type=jnp.float32
    )
    return summed.astype(jnp.bfloat16).reshape(rows_here, HEADS * HEAD)


def body(
    hidden,
    norm_gain,
    gate_weights,
    routes,
    replica_pick,
    trainer_experts,
    hot_experts,
    replica_hot,
    w_gate,
    w_up,
    w_down,
    queries,
    key_cache,
    value_cache,
    new_keys,
    new_values,
    cache_lengths,
):
    ep_count = lax.axis_size("ep")
    my_device = lax.axis_index("ep")
    device_ids = jnp.arange(ep_count, dtype=jnp.int32)
    expert_count = trainer_experts.shape[0]
    expert_ids = jnp.arange(expert_count, dtype=jnp.int32)
    hot_count = hot_experts.shape[0]
    hot_ids = jnp.arange(hot_count, dtype=jnp.int32)
    home_device = jnp.sum(
        jnp.where(trainer_experts[None, :] == expert_ids[:, None], device_ids[None, :], 0), axis=1
    )
    hosted = jnp.sum(
        jnp.where(replica_hot[:, None] == hot_ids[None, :], hot_experts[None, :], 0), axis=1
    )
    is_replica = (hosted[None, :] == expert_ids[:, None]).astype(jnp.int32)
    replica_order = jnp.cumsum(is_replica, axis=1) * is_replica
    copies = 1 + jnp.sum(is_replica, axis=1)
    my_hot = jnp.sum(jnp.where(device_ids == my_device, replica_hot, 0))
    own_pair = jnp.concatenate([w_gate, w_up], axis=0)
    own_full_pair, own_full_down = (
        lax.all_gather(own_pair, "dp", axis=1, tiled=True),
        lax.all_gather(w_down, "dp", axis=2, tiled=True),
    )
    replica_pair = jnp.zeros_like(own_pair)
    replica_down = jnp.zeros_like(w_down)
    for hot_index in range(hot_count):
        hot_expert = jnp.sum(jnp.where(hot_ids == hot_index, hot_experts, 0))
        root_device = jnp.sum(jnp.where(expert_ids == hot_expert, home_device, 0))
        sent_pair, sent_down = (
            spread(own_pair, "ep", root_device),
            spread(w_down, "ep", root_device),
        )
        wanted = my_hot == hot_index
        replica_pair = jnp.where(wanted, sent_pair, replica_pair)
        replica_down = jnp.where(wanted, sent_down, replica_down)
    replica_full_pair, replica_full_down = (
        lax.all_gather(replica_pair, "dp", axis=1, tiled=True),
        lax.all_gather(replica_down, "dp", axis=2, tiled=True),
    )
    slot_pair = jnp.stack([own_full_pair, replica_full_pair])
    slot_down = jnp.concatenate([own_full_down, replica_full_down], axis=0)
    tokens_here = hidden.shape[1]
    width = hidden.shape[2]
    entries = tokens_here * TOP
    slot_total = ep_count * SLOTS
    buffer_rows = slot_total * CAP
    entry_ids = jnp.arange(entries, dtype=jnp.int32)
    token_map = (
        (entry_ids // TOP)[:, None] == jnp.arange(tokens_here, dtype=jnp.int32)[None, :]
    ).astype(jnp.float32)
    contract_first = (((0,), (0,)), ((), ()))
    mixed_steps = []
    context_steps = []
    for step_index in range(hidden.shape[0]):
        context_steps.append(
            attend(
                queries[step_index],
                key_cache,
                value_cache,
                new_keys,
                new_values,
                cache_lengths,
                step_index,
            )
        )
        normed = scaled_norm(hidden[step_index], norm_gain)
        weights_top = gate_weights[step_index]
        gates = (weights_top / jnp.sum(weights_top, axis=-1, keepdims=True)).astype(jnp.bfloat16)
        chosen = routes[step_index].reshape(entries)
        replica_picks = replica_pick[step_index].reshape(entries)
        expert_onehot = (chosen[:, None] == expert_ids[None, :]).astype(jnp.int32)
        replica_index = replica_picks % table_lookup(expert_onehot, copies)
        order_rows = table_lookup(expert_onehot, replica_order)
        replica_device = jnp.sum(
            jnp.where(order_rows == replica_index[:, None], device_ids[None, :], 0), axis=1
        )
        target = jnp.where(
            replica_index == 0, table_lookup(expert_onehot, home_device), replica_device
        )
        second_slot = (replica_index > 0).astype(jnp.int32)
        slot_index = target * SLOTS + second_slot
        slot_onehot = (
            slot_index[:, None] == jnp.arange(slot_total, dtype=jnp.int32)[None, :]
        ).astype(jnp.int32)
        slot_rank = jnp.sum(jnp.cumsum(slot_onehot, axis=0) * slot_onehot, axis=1) - 1
        is_kept = slot_rank < CAP
        row_index = second_slot * (ep_count * CAP) + target * CAP + slot_rank
        placed = (
            is_kept[:, None]
            & (row_index[:, None] == jnp.arange(buffer_rows, dtype=jnp.int32)[None, :])
        ).astype(jnp.float32)
        dispatch = lax.dot_general(placed, token_map, contract_first).astype(jnp.bfloat16)
        weighted = placed * gates.reshape(entries).astype(jnp.float32)[:, None]
        combine_map = lax.dot_general(token_map, weighted, contract_first).astype(jnp.bfloat16)
        outgoing = jnp.dot(dispatch, normed, preferred_element_type=jnp.float32).astype(
            jnp.bfloat16
        )
        outgoing = outgoing.reshape(SLOTS, ep_count, CAP, width)
        incoming = lax.all_to_all(outgoing, "ep", split_axis=1, concat_axis=1, tiled=True)
        slot_rows = incoming.reshape(SLOTS, ep_count * CAP, width)
        projected = jnp.einsum(
            "snd,skdf->sknf", slot_rows, slot_pair, preferred_element_type=jnp.float32
        )
        hidden_units = (jax.nn.silu(projected[:, 0]) * projected[:, 1]).astype(jnp.bfloat16)
        expert_out = jnp.einsum(
            "snf,sfd->snd", hidden_units, slot_down, preferred_element_type=jnp.float32
        ).astype(jnp.bfloat16)
        expert_out = expert_out.reshape(SLOTS, ep_count, CAP, width)
        returned = lax.all_to_all(
            expert_out, "ep", split_axis=1, concat_axis=1, tiled=True
        ).reshape(buffer_rows, width)
        mixed_rows = hidden[step_index].astype(jnp.float32) + jnp.dot(
            combine_map, returned, preferred_element_type=jnp.float32
        )
        mixed_steps.append(mixed_rows.astype(jnp.bfloat16))
    return (jnp.stack(mixed_steps), jnp.stack(context_steps))


def solution(mesh):
    return jax.shard_map(
        body,
        mesh=mesh,
        in_specs=(
            P(None, ("ep", "dp"), None),
            P(),
            P(None, ("ep", "dp"), None),
            P(None, ("ep", "dp"), None),
            P(None, ("ep", "dp"), None),
            P(),
            P(),
            P(),
            P("ep", "dp", None),
            P("ep", "dp", None),
            P("ep", None, "dp"),
            P(None, ("ep", "dp"), None),
            P(("ep", "dp"), None, None),
            P(("ep", "dp"), None, None),
            P(None, ("ep", "dp"), None),
            P(None, ("ep", "dp"), None),
            P(("ep", "dp")),
        ),
        out_specs=(P(None, ("ep", "dp"), None), P(None, ("ep", "dp"), None)),
        check_vma=False,
    )
```

profile of v0, /device:TPU:0, one launch (start us, length us, event | category | flops | bytes accessed | tf_op | source)
XLA Modules:
  0.0 346.7 jit_solution(13511546393007678465)
XLA Ops:
  8.1 1.5 fusion.144
  9.5 0.8 select_reduce_fusion.4
  10.3 2.7 fusion.145
  14.9 1.2 constant_dynamic-update-slice_fusion.1
  16.1 1.3 constant_dynamic-update-slice_fusion
  17.4 2.3 broadcast_select_fusion
  20.1 1.5 broadcast_select_fusion.3
  21.6 0.5 all-gather.9.cloned.1.call-update
  22.2 0.6 fusion.139
  25.1 0.6 fusion.171
  27.1 148.3 %all-reduce.3.cloned.1.call-done = (bf16[1,384,1024]{2,1,0:T(8,128)(2,1)}, bf16[1,384,1024]{2,1,0:T(8,128)(2,1)}, bf16[1,384,1024]{2,1,0:T(8,128)(2,1)}, bf16[2,...) async-done(((bf16[1,384,1024]{2,1,0:T(8,128)(2,1)}, bf16[1,384,1024]{2,1,0:T(8,128)(2,1)}, bf16[1,384,1024]{2,1,0:T(8,128)(2,1)}, ...) | async-done | bytes 7077904 | tf_op jit(solution)/shard_map/psum | solution.py:21
  175.4 2.1 select_select_fusion.1
  177.6 0.6 reduce-window.14
  178.7 0.5 add_rsqrt_fusion
  179.3 0.6 copy-done.12
  179.8 0.6 convolution_convert_fusion.3
  180.8 1.2 copy.85
  182.0 5.0 %all-to-all-start = ((bf16[2,16,3,2048]{3,0,2,1:T(2,128)(2,1)}), bf16[2,16,3,2048]{3,0,2,1:T(2,128)(2,1)S(1)}, u32[]{:S(2)}, u32[]{:S(2)}) async-start(bf16[2,16,3,2048]{3,0,2,1:T(2,128)(2,1)} %copy.85), calls=%async_computation | async-start | bytes 786432 | tf_op jit(solution)/shard_map/all_to_all | solution.py:192
  187.1 0.5 all-gather.5.cloned.1.call-update
  189.6 0.6 reduce-window.16
  190.6 0.6 convolution_convert_fusion.1
  191.4 1.2 copy.94
  192.6 0.7 iota_compare_fusion.23
  193.4 2.9 select_select_fusion
  196.7 0.8 select_reduce_fusion.1
  197.5 1.2 select_reduce_fusion.2
  198.7 0.8 fusion.23
  199.6 0.5 fusion.168
  201.5 0.5 fusion.6
  202.5 2.7 constant_dynamic-update-slice_fusion.3
  205.3 2.8 constant_dynamic-update-slice_fusion.2
  208.1 6.0 %all-to-all-start.2 = ((bf16[2,16,3,2048]{3,0,2,1:T(2,128)(2,1)}), bf16[2,16,3,2048]{3,0,2,1:T(2,128)(2,1)S(1)}, u32[]{:S(2)}, u32[]{:S(2)}) async-start(bf16[2,16,3,2048]{3,0,2,1:T(2,128)(2,1)} %copy.94), calls=%async_computation.2 | async-start | bytes 786432 | tf_op jit(solution)/shard_map/all_to_all | solution.py:192
  214.1 37.0 %all-gather.5.cloned.1.call-done = bf16[2,2048,384]{2,1,0:T(8,128)(2,1)} async-done(((bf16[2,1024,384]{2,1,0:T(8,128)(2,1)}), bf16[2,2048,384]{2,1,0:T(8,128)(2,1)}) %all-gather.5.cloned.1.call-update) | async-done | bytes 3145744 | tf_op jit(solution)/shard_map/all_gather | solution.py:114
  251.1 46.4 %all-gather.7.cloned.1.call-done = bf16[2,2048,384]{2,1,0:T(8,128)(2,1)} async-done(((bf16[2,1024,384]{2,1,0:T(8,128)(2,1)}), bf16[2,2048,384]{2,1,0:T(8,128)(2,1)}) %all-gather.7.cloned.1.call-update) | async-done | bytes 3145744 | tf_op jit(solution)/shard_map/all_gather | solution.py:130
  297.5 3.6 %convolution_bitcast_fusion = f32[2,2,48,384]{3,2,1,0:T(8,128)S(1)} fusion(bf16[2,48,2048,1]{2,0,1,3:T(2,128)(2,1)S(1)} %bitcast.161, bf16[1,2,2048,384]{3,2,1,0:T(8,128)(2,1)} %bitcast.175, bf16[1,2,2048,384]{3,2,1,0:T(8,128)(2,1)} %bitcast.173), kind=kOutput, calls=%fused_computation.24 | convolution fusion | flops 314572800 | bytes 6979584 | tf_op jit(solution)/shard_map/snd,skdf->sknf/dot_general | solution.py:194
  301.2 0.6 convolution_convert_fusion.2
  301.9 1.2 copy.88
  303.0 5.6 %all-to-all-start.1 = ((bf16[2,16,3,2048]{3,0,2,1:T(2,128)(2,1)}), bf16[2,16,3,2048]{3,0,2,1:T(2,128)(2,1)S(1)}, u32[]{:S(2)}, u32[]{:S(2)}) async-start(bf16[2,16,3,2048]{3,0,2,1:T(2,128)(2,1)} %bitcast.15), calls=%async_computation.1 | async-start | bytes 786432 | tf_op jit(solution)/shard_map/all_to_all | solution.py:202
  308.7 3.6 %fusion.8 = f32[2,2,48,384]{3,2,0,1:T(8,128)S(1)} fusion(bf16[2,48,2048]{2,0,1:T(2,128)(2,1)S(1)} %bitcast.162, bf16[1,2,2048,384]{3,2,1,0:T(8,128)(2,1)} %bitcast.176, bf16[1,2,2048,384]{3,2,1,0:T(8,128)(2,1)} %bitcast.174), kind=kOutput, calls=%fused_computation.23 | convolution fusion | flops 305135616 | bytes 6979584 | tf_op jit(solution)/shard_map/snd,skdf->sknf/dot_general | solution.py:194
  312.4 0.7 convolution_convert_fusion
  313.1 1.2 copy.97
  314.2 6.6 %all-to-all-done.1 = bf16[2,16,3,2048]{3,0,2,1:T(2,128)(2,1)S(1)} async-done(((bf16[2,16,3,2048]{3,0,2,1:T(2,128)(2,1)}), bf16[2,16,3,2048]{3,0,2,1:T(2,128)(2,1)S(1)}, u32[]{:S(2)}, u32[]{:S(2)}) %all-to-all-start.1) | async-done | bytes 393248 | tf_op jit(solution)/shard_map/all_to_all | solution.py:202
  320.8 3.7 %all-to-all-start.3 = ((bf16[2,16,3,2048]{3,0,2,1:T(2,128)(2,1)}), bf16[2,16,3,2048]{3,0,2,1:T(2,128)(2,1)S(1)}, u32[]{:S(2)}, u32[]{:S(2)}) async-start(bf16[2,16,3,2048]{3,0,2,1:T(2,128)(2,1)} %bitcast.30), calls=%async_computation.3 | async-start | bytes 786432 | tf_op jit(solution)/shard_map/all_to_all | solution.py:202
  325.1 0.8 pad_maximum_fusion.1
  326.6 10.1 %all-to-all-done.3 = bf16[2,16,3,2048]{3,0,2,1:T(2,128)(2,1)S(1)} async-done(((bf16[2,16,3,2048]{3,0,2,1:T(2,128)(2,1)}), bf16[2,16,3,2048]{3,0,2,1:T(2,128)(2,1)S(1)}, u32[]{:S(2)}, u32[]{:S(2)}) %all-to-all-start.3) | async-done | bytes 393248 | tf_op jit(solution)/shard_map/all_to_all | solution.py:202
  337.3 0.5 fusion.5
  337.8 0.5 fusion.4
  338.4 0.7 pad_maximum_fusion.2
  (148 shorter events, 9.8 us)
Async XLA Ops:
  8.0 193.5 %copy-start = (bf16[32,32,512]{2,1,0:T(8,128)(2,1)S(1)}, bf16[32,32,512]{2,1,0:T(8,128)(2,1)}, u32[]{:S(2)}) copy-start(bf16[32,32,512]{2,1,0:T(8,128)(2,1)} %param.30) | copy-start | bytes 3145732
  8.0 167.4 %all-reduce.3.cloned.1.call-start = ((), (), s32[]{:S(2)}) async-start(), calls=%async_computation.8 | async-start | bytes 14155776 | tf_op jit(solution)/shard_map/psum | solution.py:21
  10.3 16.5 %copy-start.23 = (s32[16]{0:T(128)}, s32[16]{0:T(128)S(1)}, u32[]{:S(2)}) copy-start(s32[16]{0:T(128)S(1)} %select_reduce_fusion.4) | copy-start | bytes 196
  17.4 2.7 copy-start.3
  17.4 2.7 copy-start.4
  21.5 0.7 copy-start.28
  21.5 1.3 copy-start.27
  21.5 3.4 copy-start.14
  21.5 3.6 %copy-start.15 = (s32[2,32,8]{1,2,0:T(8,128)S(1)}, s32[2,32,8]{1,2,0:T(8,128)}, u32[]{:S(2)}) copy-start(s32[2,32,8]{1,2,0:T(8,128)} %param.21) | copy-start | bytes 6148
  21.6 156.8 %copy-start.19 = (bf16[2048]{0:T(1024)(128)(2,1)S(1)}, bf16[2048]{0:T(1024)(128)(2,1)}, u32[]{:S(2)}) copy-start(bf16[2048]{0:T(1024)(128)(2,1)} %param.18) | copy-start | bytes 12292
  21.6 156.9 %copy-start.5 = (bf16[2,32,2048]{2,1,0:T(8,128)(2,1)S(1)}, bf16[2,32,2048]{2,1,0:T(8,128)(2,1)}, u32[]{:S(2)}) copy-start(bf16[2,32,2048]{2,1,0:T(8,128)(2,1)} %param.17) | copy-start | bytes 786436
  21.6 180.9 %all-gather.9.cloned.1.call-start = ((), (), s32[]{:S(2)}) async-start(), calls=%async_computation.6 | async-start | bytes 2359296 | tf_op jit(solution)/shard_map/all_gather | solution.py:115
  22.2 183.1 %all-gather.11.cloned.1.call-start = ((), (), s32[]{:S(2)}) async-start(), calls=%async_computation.7 | async-start | bytes 2359296 | tf_op jit(solution)/shard_map/all_gather | solution.py:131
  23.0 3.6 %copy-start.25 = (s32[16]{0:T(128)}, s32[16]{0:T(128)S(1)}, u32[]{:S(2)}) copy-start(s32[16]{0:T(128)S(1)} %select_reduce_fusion.5) | copy-start | bytes 196
  26.0 153.2 %copy-start.17 = (s32[16,16]{1,0:T(8,128)}, s32[16,16]{1,0:T(8,128)S(1)}, u32[]{:S(2)}) copy-start(s32[16,16]{1,0:T(8,128)S(1)} %reduce_window_sum.36) | copy-start | bytes 3076
  26.2 153.1 %copy-start.29 = (s32[16]{0:T(128)}, s32[16]{0:T(128)S(1)}, u32[]{:S(2)}) copy-start(s32[16]{0:T(128)S(1)} %fusion.138) | copy-start | bytes 196
  177.5 10.1 %copy-start.7 = (bf16[2,32,4096]{2,1,0:T(8,128)(2,1)S(1)}, bf16[2,32,4096]{2,1,0:T(8,128)(2,1)}, u32[]{:S(2)}) copy-start(bf16[2,32,4096]{2,1,0:T(8,128)(2,1)} %param.28) | copy-start | bytes 1572868
  178.7 0.6 copy-start.20
  179.3 0.6 copy-start.12
  179.8 7.9 %copy-start.8 = (bf16[2,32,512]{2,1,0:T(8,128)(2,1)S(1)}, bf16[2,32,512]{2,1,0:T(8,128)(2,1)}, u32[]{:S(2)}) copy-start(bf16[2,32,512]{2,1,0:T(8,128)(2,1)} %param.31) | copy-start | bytes 196612
  180.5 7.4 %copy-start.9 = (bf16[2,32,512]{2,1,0:T(8,128)(2,1)S(1)}, bf16[2,32,512]{2,1,0:T(8,128)(2,1)}, u32[]{:S(2)}) copy-start(bf16[2,32,512]{2,1,0:T(8,128)(2,1)} %param.32) | copy-start | bytes 196612
  180.7 7.2 %copy-start.16 = (f32[2,32,8]{1,2,0:T(8,128)S(1)}, f32[2,32,8]{1,2,0:T(8,128)}, u32[]{:S(2)}) copy-start(f32[2,32,8]{1,2,0:T(8,128)} %param.19) | copy-start | bytes 6148
  180.7 7.7 %copy-start.11 = (s32[1,32,8]{1,2,0:T(8,128)S(1)}, s32[1,32,8]{1,2,0:T(8,128)}, u32[]{:S(2)}) copy-start(s32[1,32,8]{1,2,0:T(8,128)} %get-tuple-element.32) | copy-start | bytes 3076
  180.7 7.9 %copy-start.30 = (s32[16]{0:T(128)S(1)}, s32[16]{0:T(128)}, u32[]{:S(2)}) copy-start(s32[16]{0:T(128)} %copy-done.29) | copy-start | bytes 196
  180.7 8.3 %copy-start.18 = (s32[16,16]{1,0:T(8,128)S(1)}, s32[16,16]{1,0:T(8,128)}, u32[]{:S(2)}) copy-start(s32[16,16]{1,0:T(8,128)} %copy-done.17) | copy-start | bytes 3076
  180.7 8.3 %copy-start.26 = (s32[16]{0:T(128)S(1)}, s32[16]{0:T(128)}, u32[]{:S(2)}) copy-start(s32[16]{0:T(128)} %copy-done.25) | copy-start | bytes 196
  180.8 8.6 %copy-start.24 = (s32[16]{0:T(128)S(1)}, s32[16]{0:T(128)}, u32[]{:S(2)}) copy-start(s32[16]{0:T(128)} %copy-done.23) | copy-start | bytes 196
  182.0 8.5 %copy-start.22 = (f32[32]{0:T(128)S(1)}, f32[32]{0:T(128)}, u32[]{:S(2)}) copy-start(f32[32]{0:T(128)} %get-tuple-element.41) | copy-start | bytes 388
  182.0 26.1 %all-to-all-start = ((bf16[2,16,3,2048]{3,0,2,1:T(2,128)(2,1)}), bf16[2,16,3,2048]{3,0,2,1:T(2,128)(2,1)S(1)}, u32[]{:S(2)}, u32[]{:S(2)}) async-start(bf16[2,16,3,2048]{3,0,2,1:T(2,128)(2,1)} %copy.85), calls=%async_computation | async-start | bytes 786432 | tf_op jit(solution)/shard_map/all_to_all | solution.py:192
  187.0 64.1 %all-gather.5.cloned.1.call-start = ((), (), s32[]{:S(2)}) async-start(), calls=%async_computation.4 | async-start | bytes 4718592 | tf_op jit(solution)/shard_map/all_gather | solution.py:114
  187.6 109.9 %all-gather.7.cloned.1.call-start = ((), (), s32[]{:S(2)}) async-start(), calls=%async_computation.5 | async-start | bytes 4718592 | tf_op jit(solution)/shard_map/all_gather | solution.py:130
  187.8 8.5 %copy-start.10 = (bf16[2,32,4,128]{3,2,1,0:T(4,128)(2,1)}, bf16[2,32,4,128]{3,2,1,0:T(4,128)(2,1)S(1)}, u32[]{:S(2)}) copy-start(bf16[2,32,4,128]{3,2,1,0:T(4,128)(2,1)S(1)} %reshape.214) | copy-start | bytes 196612
  193.4 3.3 copy-start.6
  208.1 95.0 %all-to-all-start.2 = ((bf16[2,16,3,2048]{3,0,2,1:T(2,128)(2,1)}), bf16[2,16,3,2048]{3,0,2,1:T(2,128)(2,1)S(1)}, u32[]{:S(2)}, u32[]{:S(2)}) async-start(bf16[2,16,3,2048]{3,0,2,1:T(2,128)(2,1)} %copy.94), calls=%async_computation.2 | async-start | bytes 786432 | tf_op jit(solution)/shard_map/all_to_all | solution.py:192
  297.5 3.8 %copy-start.1 = (bf16[2,384,2048]{2,1,0:T(8,128)(2,1)S(1)}, bf16[2,384,2048]{2,1,0:T(8,128)(2,1)}, u32[]{:S(2)}) copy-start(bf16[2,384,2048]{2,1,0:T(8,128)(2,1)} %constant_dynamic-update-slice_fusion.2) | copy-start | bytes 9437188
  303.0 17.8 %all-to-all-start.1 = ((bf16[2,16,3,2048]{3,0,2,1:T(2,128)(2,1)}), bf16[2,16,3,2048]{3,0,2,1:T(2,128)(2,1)S(1)}, u32[]{:S(2)}, u32[]{:S(2)}) async-start(bf16[2,16,3,2048]{3,0,2,1:T(2,128)(2,1)} %bitcast.15), calls=%async_computation.1 | async-start | bytes 786432 | tf_op jit(solution)/shard_map/all_to_all | solution.py:202
  308.7 3.8 %copy-start.2 = (bf16[2,384,2048]{2,1,0:T(8,128)(2,1)S(1)}, bf16[2,384,2048]{2,1,0:T(8,128)(2,1)}, u32[]{:S(2)}) copy-start(bf16[2,384,2048]{2,1,0:T(8,128)(2,1)} %constant_dynamic-update-slice_fusion.2) | copy-start | bytes 9437188
  320.8 16.4 %copy-start.13 = (s32[256]{0:T(256)S(1)}, s32[256]{0:T(256)}, u32[]{:S(2)}) copy-start(s32[256]{0:T(256)} %copy-done.12) | copy-start | bytes 3076
  320.8 16.5 %copy-start.21 = (pred[256]{0:T(512)(128)(4,1)S(1)}, pred[256]{0:T(512)(128)(4,1)}, u32[]{:S(2)}) copy-start(pred[256]{0:T(512)(128)(4,1)} %copy-done.20) | copy-start | bytes 772
  320.8 15.8 %all-to-all-start.3 = ((bf16[2,16,3,2048]{3,0,2,1:T(2,128)(2,1)}), bf16[2,16,3,2048]{3,0,2,1:T(2,128)(2,1)S(1)}, u32[]{:S(2)}, u32[]{:S(2)}) async-start(bf16[2,16,3,2048]{3,0,2,1:T(2,128)(2,1)} %bitcast.30), calls=%async_computation.3 | async-start | bytes 786432 | tf_op jit(solution)/shard_map/all_to_all | solution.py:202
Sparse Core Ops, SparseCore 0:
  21.7 153.6 all-reduce.2
Sparse Core Ops, SparseCore 1:
  23.6 29.7 all-gather.8
  177.7 27.2 all-gather.10
  206.3 44.7 all-gather.4
  252.7 44.7 all-gather.6
where the time goes:
time: 348 us; the launch traced here: 347 us
  waiting for transfers between devices  249 us (72%)
  other arithmetic  20.8 us (6%)
  starting transfers between devices  20.5 us (6%)
  between operations  20.2 us (6%)
  local copies, waits for them, and re-layouts  18.5 us (5%)
  matrix products  17.3 us (5%)
    psum x1, waiting for transfers between devices, spread(): return lax.psum(jnp.where(mine, shard, jnp.zeros_like(shard)), axis)  148 us
    all_gather x1, waiting for transfers between devices, body(): lax.all_gather(replica_pair, 'dp', axis=1, tiled=True)  46.4 us
    all_gather x1, waiting for transfers between devices, body(): lax.all_gather(own_pair, 'dp', axis=1, tiled=True)  37 us
    all_to_all x2, waiting for transfers between devices, body(): lax.all_to_all(expert_out, 'ep', split_axis=1, concat_axis=1, tiled=True)  16.7 us
    all_to_all x2, starting transfers between devices, body(): lax.all_to_all(outgoing, 'ep', split_axis=1, concat_axis=1, tiled=True)  11 us
    all_to_all x2, starting transfers between devices, body(): lax.all_to_all(expert_out, 'ep', split_axis=1, concat_axis=1, tiled=True)  9.3 us
    dot_general x2, matrix products, body(): jnp.einsum('snd,skdf->sknf', slot_rows, slot_pair, preferred_element_type...  7.23 us
  transfers between devices with their start and end apart: 9, of which 5 were waited for; matrix products, arithmetic and copies ran while one was open for 12% of the time, Pallas kernels for 0%

commit v1 on v0

v1 whole, which is shorter than its diff:
```python
import math

import jax
import jax.numpy as jnp
from jax import lax
from jax.sharding import PartitionSpec as P

HEADS = 32
KV_HEADS = 4
HEAD = 128
TOP = 8
CAP = 3
SLOTS = 2
LANES = 128
OUTER = 4
OUT_COLUMNS = 512
STEP_BYTES = 1 << 22

norm_epsilon = 1e-06


def scaled_norm(hidden_rows, norm_gain):
    values = hidden_rows.astype(jnp.float32)
    mean_square = jnp.mean(values * values, axis=-1, keepdims=True)
    return (values * lax.rsqrt(mean_square + norm_epsilon) * norm_gain.astype(jnp.float32)).astype(
        jnp.bfloat16
    )


def table_lookup(onehot_rows, table):
    return jnp.dot(onehot_rows, table, preferred_element_type=jnp.int32)


def attend(query_rows, key_cache, value_cache, new_keys, new_values, cache_lengths, step_index):
    rows_here = query_rows.shape[0]
    cache_len = key_cache.shape[1]
    steps_all = new_keys.shape[0]
    grouped = query_rows.reshape(rows_here, KV_HEADS, HEADS // KV_HEADS, HEAD)
    keys_cached = key_cache.reshape(rows_here, cache_len, KV_HEADS, HEAD)
    values_cached = value_cache.reshape(rows_here, cache_len, KV_HEADS, HEAD)
    keys_fresh = new_keys.reshape(steps_all, rows_here, KV_HEADS, HEAD)
    values_fresh = new_values.reshape(steps_all, rows_here, KV_HEADS, HEAD)
    score_scale = 1.0 / math.sqrt(HEAD)
    cache_scores = (
        jnp.einsum("rkgh,rckh->rkgc", grouped, keys_cached, preferred_element_type=jnp.float32)
        * score_scale
    )
    fresh_scores = (
        jnp.einsum("rkgh,srkh->rkgs", grouped, keys_fresh, preferred_element_type=jnp.float32)
        * score_scale
    )
    cache_mask = (jnp.arange(cache_len, dtype=jnp.int32)[None, :] < cache_lengths[:, None])[
        :, None, None, :
    ]
    fresh_mask = (jnp.arange(steps_all, dtype=jnp.int32) <= step_index)[None, None, None, :]
    row_max = jnp.maximum(
        jnp.max(jnp.where(cache_mask, cache_scores, -1e30), axis=-1),
        jnp.max(jnp.where(fresh_mask, fresh_scores, -1e30), axis=-1),
    )
    cache_exp = jnp.where(cache_mask, jnp.exp(cache_scores - row_max[..., None]), 0.0)
    fresh_exp = jnp.where(fresh_mask, jnp.exp(fresh_scores - row_max[..., None]), 0.0)
    row_total = jnp.sum(cache_exp, axis=-1) + jnp.sum(fresh_exp, axis=-1)
    cache_probs = (cache_exp / row_total[..., None]).astype(jnp.bfloat16)
    fresh_probs = (fresh_exp / row_total[..., None]).astype(jnp.bfloat16)
    summed = jnp.einsum(
        "rkgc,rckh->rkgh", cache_probs, values_cached, preferred_element_type=jnp.float32
    )
    summed = summed + jnp.einsum(
        "rkgs,srkh->rkgh", fresh_probs, values_fresh, preferred_element_type=jnp.float32
    )
    return summed.astype(jnp.bfloat16).reshape(rows_here, HEADS * HEAD)


def kept_gates(
    routes,
    replica_pick,
    gate_weights,
    expert_ids,
    device_ids,
    home_device,
    replica_order,
    copies,
):
    tokens_here = routes.shape[0]
    entries = tokens_here * TOP
    slot_total = device_ids.shape[0] * SLOTS
    gates = (gate_weights / jnp.sum(gate_weights, axis=-1, keepdims=True)).astype(jnp.bfloat16)
    chosen = routes.reshape(entries)
    replica_picks = replica_pick.reshape(entries)
    expert_onehot = (chosen[:, None] == expert_ids[None, :]).astype(jnp.int32)
    replica_index = replica_picks % table_lookup(expert_onehot, copies)
    order_rows = table_lookup(expert_onehot, replica_order)
    replica_device = jnp.sum(
        jnp.where(order_rows == replica_index[:, None], device_ids[None, :], 0), axis=1
    )
    target = jnp.where(replica_index == 0, table_lookup(expert_onehot, home_device), replica_device)
    slot_index = target * SLOTS + (replica_index > 0).astype(jnp.int32)
    slot_onehot = (
        slot_index[:, None] == jnp.arange(slot_total, dtype=jnp.int32)[None, :]
    ).astype(jnp.int32)
    slot_rank = jnp.sum(jnp.cumsum(slot_onehot, axis=0) * slot_onehot, axis=1) - 1
    kept = jnp.where(slot_rank < CAP, gates.reshape(entries).astype(jnp.float32), 0.0)
    spread = kept[:, None] * expert_onehot.astype(jnp.float32)
    return jnp.sum(spread.reshape(tokens_here, TOP, expert_ids.shape[0]), axis=1)


def roll_blocks(rows, start, count):
    width = rows.shape[1] // count
    twice = jnp.concatenate([rows, rows], axis=1)
    return lax.dynamic_slice_in_dim(twice, start * width, rows.shape[1], axis=1)


def swap(value, axis_size, stride):
    return lax.ppermute(value, "ep", [(i, i ^ stride) for i in range(axis_size)])


def pull(value, axis_size, inner, offset):
    outer = axis_size // inner
    return lax.ppermute(
        value,
        "ep",
        [
            (z * inner + r, (z - offset) % outer * inner + r)
            for z in range(outer)
            for r in range(inner)
        ],
    )


def gather_rows(rows, axis_size, inner):
    outer = axis_size // inner
    held = jnp.concatenate([rows] + [pull(rows, axis_size, inner, r) for r in range(1, outer)])
    stride = inner // 2
    while stride >= 1:
        held = jnp.concatenate([held, swap(held, axis_size, stride)])
        stride //= 2
    return held


def scatter_sum(values, axis_size, inner):
    outer = axis_size // inner
    stride = 1
    while stride < inner:
        half = values.shape[0] // 2
        values = values[:half] + swap(values[half:], axis_size, stride)
        stride *= 2
    rows = values.shape[0] // outer
    total = values[:rows]
    for r in range(1, outer):
        total = total + pull(values[r * rows : (r + 1) * rows], axis_size, inner, outer - r)
    return total


def one_step_at_a_time(hidden):
    return lax.axis_size("ep") * hidden.shape[1] * hidden.shape[2] * 2 > STEP_BYTES


def compute(
    hidden,
    norm_gain,
    gate_weights,
    routes,
    replica_pick,
    trainer_experts,
    hot_experts,
    replica_hot,
    w_gate,
    w_up,
    w_down,
    queries,
    key_cache,
    value_cache,
    new_keys,
    new_values,
    cache_lengths,
):
    ep_count = lax.axis_size("ep")
    dp_count = lax.axis_size("dp")
    my_device = lax.axis_index("ep")
    my_column = lax.axis_index("dp")
    inner = max(1, ep_count // OUTER)
    steps, _, width = hidden.shape
    block = width // dp_count

    def complete(shard):
        return [shard] + [
            lax.ppermute(shard, "dp", [(i, (i - s) % dp_count) for i in range(dp_count)])
            for s in range(1, dp_count)
        ]

    gate_parts = complete(w_gate[0])
    up_parts = complete(w_up[0])
    down_parts = complete(w_down[0])

    device_ids = jnp.arange(ep_count, dtype=jnp.int32)
    expert_count = trainer_experts.shape[0]
    expert_ids = jnp.arange(expert_count, dtype=jnp.int32)
    hot_ids = jnp.arange(hot_experts.shape[0], dtype=jnp.int32)
    home_device = jnp.sum(
        jnp.where(trainer_experts[None, :] == expert_ids[:, None], device_ids[None, :], 0), axis=1
    )
    hosted = jnp.sum(
        jnp.where(replica_hot[:, None] == hot_ids[None, :], hot_experts[None, :], 0), axis=1
    )
    is_replica = (hosted[None, :] == expert_ids[:, None]).astype(jnp.int32)
    replica_order = jnp.cumsum(is_replica, axis=1) * is_replica
    copies = 1 + jnp.sum(is_replica, axis=1)
    my_expert = jnp.sum(jnp.where(device_ids == my_device, trainer_experts, 0))
    lanes = -(-expert_count // LANES) * LANES

    gate_rest = jnp.concatenate(gate_parts[1:])
    up_rest = jnp.concatenate(up_parts[1:])
    span = max(1, OUT_COLUMNS // block)
    down_groups = [
        jnp.concatenate(down_parts[s : s + span], axis=1) for s in range(0, dp_count, span)
    ]
    lane = jnp.arange(lanes, dtype=jnp.int32)
    one_by_one = one_step_at_a_time(hidden)

    def prepare(step_index):
        normed = roll_blocks(scaled_norm(hidden[step_index], norm_gain), my_column, dp_count)
        kept = kept_gates(
            routes[step_index],
            replica_pick[step_index],
            gate_weights[step_index],
            expert_ids,
            device_ids,
            home_device,
            replica_order,
            copies,
        )
        kept = jnp.pad(kept.astype(jnp.bfloat16), ((0, 0), (0, lanes - expert_count)))
        return jnp.concatenate([normed, kept], axis=1)

    def process(packed):
        rows = gather_rows(packed, ep_count, inner)
        own = rows[:, :block]
        rest = rows[:, block:width]
        gate_part = jnp.dot(own, gate_parts[0], preferred_element_type=jnp.float32) + jnp.dot(
            rest, gate_rest, preferred_element_type=jnp.float32
        )
        up_part = jnp.dot(own, up_parts[0], preferred_element_type=jnp.float32) + jnp.dot(
            rest, up_rest, preferred_element_type=jnp.float32
        )
        units = (jax.nn.silu(gate_part) * up_part).astype(jnp.bfloat16)
        gate = jnp.sum(
            jnp.where(lane[None, :] == my_expert, rows[:, width:].astype(jnp.float32), 0.0),
            axis=1,
            keepdims=True,
        )
        blocks = []
        for s, down_part in enumerate(down_groups):
            if one_by_one and s:
                units, _ = lax.optimization_barrier((units, blocks[-1]))
            expert_out = jnp.dot(
                units, down_part, preferred_element_type=jnp.float32
            ).astype(jnp.bfloat16)
            weighted = gate * expert_out.astype(jnp.float32)
            blocks.append(scatter_sum(weighted, ep_count, inner))
        return jnp.concatenate(blocks, axis=1)

    if one_by_one:
        packed = jnp.stack([prepare(step_index) for step_index in range(steps)])
        sums = lax.map(lambda rows: process(rows), packed)
    else:
        sums = [process(prepare(step_index)) for step_index in range(steps)]

    context_steps = [
        attend(
            queries[step_index],
            key_cache,
            value_cache,
            new_keys,
            new_values,
            cache_lengths,
            step_index,
        )
        for step_index in range(steps)
    ]

    mixed_steps = []
    for step_index in range(steps):
        total = roll_blocks(sums[step_index], (dp_count - my_column) % dp_count, dp_count)
        mixed_steps.append(
            (hidden[step_index].astype(jnp.float32) + total).astype(jnp.bfloat16)
        )
    return (jnp.stack(mixed_steps), jnp.stack(context_steps))


def solution(mesh):
    return jax.shard_map(
        compute,
        mesh=mesh,
        in_specs=(
            P(None, ("ep", "dp"), None),
            P(),
            P(None, ("ep", "dp"), None),
            P(None, ("ep", "dp"), None),
            P(None, ("ep", "dp"), None),
            P(),
            P(),
            P(),
            P("ep", "dp", None),
            P("ep", "dp", None),
            P("ep", None, "dp"),
            P(None, ("ep", "dp"), None),
            P(("ep", "dp"), None, None),
            P(("ep", "dp"), None, None),
            P(None, ("ep", "dp"), None),
            P(None, ("ep", "dp"), None),
            P(("ep", "dp")),
        ),
        out_specs=(P(None, ("ep", "dp"), None), P(None, ("ep", "dp"), None)),
        check_vma=False,
    )
```

time: 348 us -> 188 us (0.54)
  waiting for transfers between devices: 249 us -> 74 us
  starting transfers between devices: 20.5 us -> 47.9 us
  between operations: 20.2 us -> 1.51 us
  local copies, waits for them, and re-layouts: 18.5 us -> 23.5 us
    psum x1 -> x0, waiting for transfers between devices: 148 us -> none  [spread(): return lax.psum(jnp.where(mine, shard, jnp.zeros_like(shard)), axis)]
    all_gather x4 -> x0, waiting for transfers between devices: 83.4 us -> none  [the longest x1 46.4 us: body(): lax.all_gather(replica_pair, 'dp', axis=1, tiled=True)]
    ppermute x0 -> x33, waiting for transfers between devices: none -> 74 us  [the longest x12 39.7 us: swap(): lax.ppermute(value, 'ep', [(i, i ^ stride) for i in range(axis_size)])]
    ppermute x0 -> x33, starting transfers between devices: none -> 47.9 us  [the longest x18 35.8 us: pull(): lax.ppermute(value, 'ep', [(z * inner + r, (z - offset) % outer * inner +...]
    all_to_all x4 -> x0, starting transfers between devices: 20.3 us -> none  [the longest x2 11 us: body(): lax.all_to_all(outgoing, 'ep', split_axis=1, concat_axis=1, tiled=True)]
    all_to_all x4 -> x0, waiting for transfers between devices: 16.7 us -> none  [the longest x2 16.7 us: body(): lax.all_to_all(expert_out, 'ep', split_axis=1, concat_axis=1, tiled=True)]
    select_n x7 -> x3, other arithmetic: 9.14 us -> 0.29 us  [the longest x2 0.16 us: kept_gates(): jnp.where(slot_rank < CAP, gates.reshape(entries).astype(jnp.float32), 0.0)]
    unnamed x67 -> x65, local copies, waits for them, and re-layouts: 5.35 us -> 11.9 us
  transfers between devices with their start and end apart: 9 -> 33, of which waited for: 5 -> 12; matrix products, arithmetic and copies ran while one was open for 12% -> 25% of each run, Pallas kernels for 0% -> 0%
where the time goes in v1:
time: 188 us; the launch traced here: 187 us
  waiting for transfers between devices  74 us (39%)
  starting transfers between devices  47.9 us (25%)
  local copies, waits for them, and re-layouts  23.5 us (12%)
  other arithmetic  22 us (12%)
  matrix products  18.3 us (10%)
    ppermute x12, waiting for transfers between devices, swap(): lax.ppermute(value, 'ep', [(i, i ^ stride) for i in range(axis_size)])  39.7 us
    ppermute x18, starting transfers between devices, pull(): lax.ppermute(value, 'ep', [(z * inner + r, (z - offset) % outer * inner +...  35.8 us
    ppermute x18, waiting for transfers between devices, pull(): lax.ppermute(value, 'ep', [(z * inner + r, (z - offset) % outer * inner +...  18.4 us
    ppermute x3, waiting for transfers between devices, complete(): lax.ppermute(shard, 'dp', [(i, (i - s) % dp_count) for i in range(dp_coun...  15.9 us
    unnamed x65, local copies, waits for them, and re-layouts  11.9 us
    ppermute x12, starting transfers between devices, swap(): lax.ppermute(value, 'ep', [(i, i ^ stride) for i in range(axis_size)])  8.44 us
    add x8, other arithmetic, scatter_sum(): values = values[:half] + swap(values[half:], axis_size, stride)  6.02 us
    dot_general x4, matrix products, process(): jnp.dot(units, down_part, preferred_element_type=jnp.float32)  5.15 us
  transfers between devices with their start and end apart: 33, of which 12 were waited for; matrix products, arithmetic and copies ran while one was open for 25% of the time, Pallas kernels for 0%

profile of v1, /device:TPU:0, one launch (start us, length us, event | category | flops | bytes accessed | tf_op | source)
XLA Modules:
  0.0 187.2 jit_solution(16764324528289670491)
XLA Ops:
  8.7 1.1 fusion.28
  9.9 1.1 fusion.30
  11.9 5.1 %collective-permute-start = (bf16[32,2176]{1,0:T(8,128)(2,1)}, bf16[32,2176]{1,0:T(8,128)(2,1)}, u32[]{:S(2)}, u32[]{:S(2)}) collective-permute-start(bf16[32,2176]{1,0:T(8,128)(2,1)} %get-tuple-element.40), channel_id=1, source_target_pairs={{0,24},{2,26},{4,28},{6,30},{8,0},{10,2},{12,4},{14,6},{16,8},{18,... | collective-permute-start | bytes 417800 | tf_op jit(solution)/shard_map/ppermute | solution.py:119
  21.0 2.8 %collective-permute-start.18 = (bf16[32,2176]{1,0:T(8,128)(2,1)}, bf16[32,2176]{1,0:T(8,128)(2,1)}, u32[]{:S(2)}, u32[]{:S(2)}) collective-permute-start(bf16[32,2176]{1,0:T(8,128)(2,1)} %get-tuple-element.49), channel_id=1, source_target_pairs={{0,24},{2,26},{4,28},{6,30},{8,0},{10,2},{12,4},{14,6},{16,8},{18,... | collective-permute-start | bytes 417800 | tf_op jit(solution)/shard_map/ppermute | solution.py:119
  23.8 1.1 collective-permute-start.19
  28.4 1.2 select_reduce_fusion.4
  29.6 1.5 fusion.26
  36.8 1.6 collective-permute-start.5
  40.0 1.6 collective-permute-start.12
  41.5 1.5 collective-permute-start.3
  44.9 1.6 collective-permute-start.21
  46.5 1.6 constant_dynamic-update-slice_fusion.3
  48.0 1.6 constant_dynamic-update-slice_fusion.2
  50.3 6.7 %collective-permute-done.3 = bf16[128,2176]{1,0:T(8,128)(2,1)S(1)} collective-permute-done((bf16[128,2176]{1,0:T(8,128)(2,1)S(1)}, bf16[128,2176]{1,0:T(8,128)(2,1)S(1)}, u32[]{:S(2)}, u32[]{:S(2)}) %collective-permute-start.3) | collective-permute-done | bytes 557088 | tf_op jit(solution)/shard_map/ppermute | solution.py:114
  57.9 1.6 constant_dynamic-update-slice_fusion.14
  59.5 1.6 constant_dynamic-update-slice_fusion.13
  61.8 3.8 %collective-permute-done.21 = bf16[128,2176]{1,0:T(8,128)(2,1)S(1)} collective-permute-done((bf16[128,2176]{1,0:T(8,128)(2,1)S(1)}, bf16[128,2176]{1,0:T(8,128)(2,1)S(1)}, u32[]{:S(2)}, u32[]{:S(2)}) %collective-permute-start.21) | collective-permute-done | bytes 557088 | tf_op jit(solution)/shard_map/ppermute | solution.py:114
  67.4 6.8 %collective-permute-done.6 = bf16[1024,384]{1,0:T(8,128)(2,1)S(1)} collective-permute-done((bf16[1024,384]{1,0:T(8,128)(2,1)}, bf16[1024,384]{1,0:T(8,128)(2,1)S(1)}, u32[]{:S(2)}, u32[]{:S(2)}) %collective-permute-start.6) | collective-permute-done | bytes 786464 | tf_op jit(solution)/shard_map/ppermute | solution.py:187
  77.5 1.8 convert_multiply_fusion.3
  79.4 9.1 %collective-permute-done.12 = bf16[384,1024]{1,0:T(8,128)(2,1)S(1)} collective-permute-done((bf16[384,1024]{1,0:T(8,128)(2,1)}, bf16[384,1024]{1,0:T(8,128)(2,1)S(1)}, u32[]{:S(2)}, u32[]{:S(2)}) %collective-permute-start.12) | collective-permute-done | bytes 786464 | tf_op jit(solution)/shard_map/ppermute | solution.py:187
  89.2 1.2 slice.223
  95.7 1.3 slice.243
  97.3 1.9 %convert_multiply_fusion.1 = f32[512,1024]{1,0:T(8,128)S(1)} fusion(bf16[512,384]{1,0:T(8,128)(2,1)S(1)} %multiply_convert_fusion, f32[512]{0:T(512)S(1)} %get-tuple-element.9, bf16[1,384,1024]{2,1,0:T(8,128)(2,1)} %param.27), kind=kOutput, calls=%fused_computation.1 | convolution fusion | flops 404226048 | bytes 3278848 | tf_op jit(solution)/shard_map/dot_general | solution.py:255
  99.2 1.3 copy-done.1
  100.5 1.1 slice.235
  102.9 1.7 slice_add_fusion.2
  104.7 1.6 collective-permute-start.14
  106.3 1.4 slice_add_fusion.3
  108.3 1.4 slice_add_fusion
  109.7 1.5 collective-permute-start.29
  111.3 1.4 slice_add_fusion.1
  113.3 6.2 %collective-permute-done.14 = f32[128,1024]{1,0:T(8,128)S(1)} collective-permute-done((f32[128,1024]{1,0:T(8,128)S(1)}, f32[128,1024]{1,0:T(8,128)S(1)}, u32[]{:S(2)}, u32[]{:S(2)}) %collective-permute-start.14) | collective-permute-done | bytes 524320 | tf_op jit(solution)/shard_map/ppermute | solution.py:114
  119.6 3.5 %collective-permute-start.17 = (f32[32,1024]{1,0:T(8,128)S(1)}, f32[32,1024]{1,0:T(8,128)S(1)}, u32[]{:S(2)}, u32[]{:S(2)}) collective-permute-start(f32[32,1024]{1,0:T(8,128)S(1)} %get-tuple-element.20), channel_id=1, source_target_pairs={{0,24},{2,26},{4,28},{6,30},{8,0},{10,2},{12,4},{14,6},{16,8},{18,... | collective-permute-start | bytes 393224 | tf_op jit(solution)/shard_map/ppermute | solution.py:119
  123.4 7.4 %collective-permute-done.8 = f32[128,1024]{1,0:T(8,128)S(1)} collective-permute-done((f32[128,1024]{1,0:T(8,128)S(1)}, f32[128,1024]{1,0:T(8,128)S(1)}, u32[]{:S(2)}, u32[]{:S(2)}) %collective-permute-start.8) | collective-permute-done | bytes 524320 | tf_op jit(solution)/shard_map/ppermute | solution.py:114
  130.8 2.3 %collective-permute-start.15 = (f32[32,1024]{1,0:T(8,128)S(1)}, f32[32,1024]{1,0:T(8,128)S(1)}, u32[]{:S(2)}, u32[]{:S(2)}) collective-permute-start(f32[32,1024]{1,0:T(8,128)S(1)} %get-tuple-element.19), channel_id=1, source_target_pairs={{0,8},{2,10},{4,12},{6,14},{8,16},{10,18},{12,20},{14,22},{16,24},... | collective-permute-start | bytes 393224 | tf_op jit(solution)/shard_map/ppermute | solution.py:119
  133.1 8.9 %collective-permute-done.29 = f32[128,1024]{1,0:T(8,128)S(1)} collective-permute-done((f32[128,1024]{1,0:T(8,128)S(1)}, f32[128,1024]{1,0:T(8,128)S(1)}, u32[]{:S(2)}, u32[]{:S(2)}) %collective-permute-start.29) | collective-permute-done | bytes 524320 | tf_op jit(solution)/shard_map/ppermute | solution.py:114
  142.0 3.5 %collective-permute-start.11 = (f32[32,1024]{1,0:T(8,128)S(1)}, f32[32,1024]{1,0:T(8,128)S(1)}, u32[]{:S(2)}, u32[]{:S(2)}) collective-permute-start(f32[32,1024]{1,0:T(8,128)S(1)} %get-tuple-element.17), channel_id=1, source_target_pairs={{0,24},{2,26},{4,28},{6,30},{8,0},{10,2},{12,4},{14,6},{16,8},{18,... | collective-permute-start | bytes 393224 | tf_op jit(solution)/shard_map/ppermute | solution.py:119
  145.6 6.8 %collective-permute-done.24 = f32[128,1024]{1,0:T(8,128)S(1)} collective-permute-done((f32[128,1024]{1,0:T(8,128)S(1)}, f32[128,1024]{1,0:T(8,128)S(1)}, u32[]{:S(2)}, u32[]{:S(2)}) %collective-permute-start.24) | collective-permute-done | bytes 524320 | tf_op jit(solution)/shard_map/ppermute | solution.py:114
  152.3 2.1 %collective-permute-start.10 = (f32[32,1024]{1,0:T(8,128)S(1)}, f32[32,1024]{1,0:T(8,128)S(1)}, u32[]{:S(2)}, u32[]{:S(2)}) collective-permute-start(f32[32,1024]{1,0:T(8,128)S(1)} %get-tuple-element.18), channel_id=1, source_target_pairs={{0,16},{2,18},{4,20},{6,22},{8,24},{10,26},{12,28},{14,30},{16,0},... | collective-permute-start | bytes 393224 | tf_op jit(solution)/shard_map/ppermute | solution.py:119
  154.5 2.0 %collective-permute-start.9 = (f32[32,1024]{1,0:T(8,128)S(1)}, f32[32,1024]{1,0:T(8,128)S(1)}, u32[]{:S(2)}, u32[]{:S(2)}) collective-permute-start(f32[32,1024]{1,0:T(8,128)S(1)} %get-tuple-element.16), channel_id=1, source_target_pairs={{0,8},{2,10},{4,12},{6,14},{8,16},{10,18},{12,20},{14,22},{16,24},... | collective-permute-start | bytes 393224 | tf_op jit(solution)/shard_map/ppermute | solution.py:119
  156.5 1.9 %collective-permute-start.32 = (f32[32,1024]{1,0:T(8,128)S(1)}, f32[32,1024]{1,0:T(8,128)S(1)}, u32[]{:S(2)}, u32[]{:S(2)}) collective-permute-start(f32[32,1024]{1,0:T(8,128)S(1)} %get-tuple-element.26), channel_id=1, source_target_pairs={{0,24},{2,26},{4,28},{6,30},{8,0},{10,2},{12,4},{14,6},{16,8},{18,... | collective-permute-start | bytes 393224 | tf_op jit(solution)/shard_map/ppermute | solution.py:119
  158.5 1.4 collective-permute-start.30
  159.8 6.9 %collective-permute-done.10 = f32[32,1024]{1,0:T(8,128)S(1)} collective-permute-done((f32[32,1024]{1,0:T(8,128)S(1)}, f32[32,1024]{1,0:T(8,128)S(1)}, u32[]{:S(2)}, u32[]{:S(2)}) %collective-permute-start.10) | collective-permute-done | bytes 131104 | tf_op jit(solution)/shard_map/ppermute | solution.py:119
  166.7 2.0 %collective-permute-start.27 = (f32[32,1024]{1,0:T(8,128)S(1)}, f32[32,1024]{1,0:T(8,128)S(1)}, u32[]{:S(2)}, u32[]{:S(2)}) collective-permute-start(f32[32,1024]{1,0:T(8,128)S(1)} %get-tuple-element.23), channel_id=1, source_target_pairs={{0,24},{2,26},{4,28},{6,30},{8,0},{10,2},{12,4},{14,6},{16,8},{18,... | collective-permute-start | bytes 393224 | tf_op jit(solution)/shard_map/ppermute | solution.py:119
  168.7 4.4 %collective-permute-start.26 = (f32[32,1024]{1,0:T(8,128)S(1)}, f32[32,1024]{1,0:T(8,128)S(1)}, u32[]{:S(2)}, u32[]{:S(2)}) collective-permute-start(f32[32,1024]{1,0:T(8,128)S(1)} %get-tuple-element.24), channel_id=1, source_target_pairs={{0,16},{2,18},{4,20},{6,22},{8,24},{10,26},{12,28},{14,30},{16,0},... | collective-permute-start | bytes 393224 | tf_op jit(solution)/shard_map/ppermute | solution.py:119
  173.2 2.3 %collective-permute-start.25 = (f32[32,1024]{1,0:T(8,128)S(1)}, f32[32,1024]{1,0:T(8,128)S(1)}, u32[]{:S(2)}, u32[]{:S(2)}) collective-permute-start(f32[32,1024]{1,0:T(8,128)S(1)} %get-tuple-element.22), channel_id=1, source_target_pairs={{0,8},{2,10},{4,12},{6,14},{8,16},{10,18},{12,20},{14,22},{16,24},... | collective-permute-start | bytes 393224 | tf_op jit(solution)/shard_map/ppermute | solution.py:119
  175.5 6.5 %collective-permute-done.31 = f32[32,1024]{1,0:T(8,128)S(1)} collective-permute-done((f32[32,1024]{1,0:T(8,128)S(1)}, f32[32,1024]{1,0:T(8,128)S(1)}, u32[]{:S(2)}, u32[]{:S(2)}) %collective-permute-start.31) | collective-permute-done | bytes 131104 | tf_op jit(solution)/shard_map/ppermute | solution.py:119
  182.0 4.2 %collective-permute-done.26 = f32[32,1024]{1,0:T(8,128)S(1)} collective-permute-done((f32[32,1024]{1,0:T(8,128)S(1)}, f32[32,1024]{1,0:T(8,128)S(1)}, u32[]{:S(2)}, u32[]{:S(2)}) %collective-permute-start.26) | collective-permute-done | bytes 131104 | tf_op jit(solution)/shard_map/ppermute | solution.py:119
  (209 shorter events, 43.2 us)
Async XLA Ops:
  0.6 32.4 %copy-start = (bf16[32,32,512]{2,1,0:T(8,128)(2,1)S(1)}, bf16[32,32,512]{2,1,0:T(8,128)(2,1)}, u32[]{:S(2)}) copy-start(bf16[32,32,512]{2,1,0:T(8,128)(2,1)} %param.30) | copy-start | bytes 3145732
  0.6 24.3 %copy-start.19 = (s32[32]{0:T(128)S(1)}, s32[32]{0:T(128)}, u32[]{:S(2)}) copy-start(s32[32]{0:T(128)} %param.33) | copy-start | bytes 388
  9.9 16.3 %copy-start.15 = (bf16[2,32,512]{2,1,0:T(8,128)(2,1)S(1)}, bf16[2,32,512]{2,1,0:T(8,128)(2,1)}, u32[]{:S(2)}) copy-start(bf16[2,32,512]{2,1,0:T(8,128)(2,1)} %param.31) | copy-start | bytes 196612
  11.1 16.0 %copy-start.9 = (bf16[32,32,512]{2,1,0:T(8,128)(2,1)S(1)}, bf16[32,32,512]{2,1,0:T(8,128)(2,1)}, u32[]{:S(2)}) copy-start(bf16[32,32,512]{2,1,0:T(8,128)(2,1)} %param.29) | copy-start | bytes 3145732
  11.9 24.6 %collective-permute-start = (bf16[32,2176]{1,0:T(8,128)(2,1)}, bf16[32,2176]{1,0:T(8,128)(2,1)}, u32[]{:S(2)}, u32[]{:S(2)}) collective-permute-start(bf16[32,2176]{1,0:T(8,128)(2,1)} %get-tuple-element.40), channel_id=1, source_target_pairs={{0,24},{2,26},{4,28},{6,30},{8,0},{10,2},{12,4},{14,6},{16,8},{18,... | collective-permute-start | bytes 417800 | tf_op jit(solution)/shard_map/ppermute | solution.py:119
  17.0 19.8 %collective-permute-start.1 = (bf16[32,2176]{1,0:T(8,128)(2,1)}, bf16[32,2176]{1,0:T(8,128)(2,1)}, u32[]{:S(2)}, u32[]{:S(2)}) collective-permute-start(bf16[32,2176]{1,0:T(8,128)(2,1)} %get-tuple-element.40), channel_id=1, source_target_pairs={{0,16},{2,18},{4,20},{6,22},{8,24},{10,26},{12,28},{14,30},{16,0},... | collective-permute-start | bytes 417800 | tf_op jit(solution)/shard_map/ppermute | solution.py:119
  17.0 21.4 %collective-permute-start.2 = (bf16[32,2176]{1,0:T(8,128)(2,1)}, bf16[32,2176]{1,0:T(8,128)(2,1)S(1)}, u32[]{:S(2)}, u32[]{:S(2)}) collective-permute-start(bf16[32,2176]{1,0:T(8,128)(2,1)} %get-tuple-element.40), channel_id=1, source_target_pairs={{0,8},{2,10},{4,12},{6,14},{8,16},{10,18},{12,20},{14,22},{16,24},... | collective-permute-start | bytes 417800 | tf_op jit(solution)/shard_map/ppermute | solution.py:119
  20.0 7.9 %copy-start.13 = (bf16[32,128]{1,0:T(8,128)(2,1)}, bf16[32,128]{1,0:T(8,128)(2,1)S(1)}, u32[]{:S(2)}) copy-start(bf16[32,128]{1,0:T(8,128)(2,1)S(1)} %pad.8.clone) | copy-start | bytes 24580
  21.0 19.0 %collective-permute-start.18 = (bf16[32,2176]{1,0:T(8,128)(2,1)}, bf16[32,2176]{1,0:T(8,128)(2,1)}, u32[]{:S(2)}, u32[]{:S(2)}) collective-permute-start(bf16[32,2176]{1,0:T(8,128)(2,1)} %get-tuple-element.49), channel_id=1, source_target_pairs={{0,24},{2,26},{4,28},{6,30},{8,0},{10,2},{12,4},{14,6},{16,8},{18,... | collective-permute-start | bytes 417800 | tf_op jit(solution)/shard_map/ppermute | solution.py:119
  23.8 17.8 %collective-permute-start.19 = (bf16[32,2176]{1,0:T(8,128)(2,1)}, bf16[32,2176]{1,0:T(8,128)(2,1)}, u32[]{:S(2)}, u32[]{:S(2)}) collective-permute-start(bf16[32,2176]{1,0:T(8,128)(2,1)} %get-tuple-element.49), channel_id=1, source_target_pairs={{0,16},{2,18},{4,20},{6,22},{8,24},{10,26},{12,28},{14,30},{16,0},... | collective-permute-start | bytes 417800 | tf_op jit(solution)/shard_map/ppermute | solution.py:119
  24.9 3.0 %copy-start.20 = (pred[2]{0:T(512)(128)(4,1)}, pred[2]{0:T(512)(128)(4,1)S(1)}, u32[]{:S(2)}) copy-start(pred[2]{0:T(512)(128)(4,1)S(1)} %iota_compare_fusion.19) | copy-start | bytes 10
  24.9 3.4 %copy-start.22 = (pred[2]{0:T(512)(128)(4,1)}, pred[2]{0:T(512)(128)(4,1)S(1)}, u32[]{:S(2)}) copy-start(pred[2]{0:T(512)(128)(4,1)S(1)} %iota_compare_fusion.18) | copy-start | bytes 10
  33.5 3.3 %copy-start.6 = (bf16[1,1024,384]{2,1,0:T(8,128)(2,1)S(1)}, bf16[1,1024,384]{2,1,0:T(8,128)(2,1)}, u32[]{:S(2)}) copy-start(bf16[1,1024,384]{2,1,0:T(8,128)(2,1)} %param.25) | copy-start | bytes 2359300
  34.2 9.7 %copy-start.14 = (bf16[32,128]{1,0:T(8,128)(2,1)S(1)}, bf16[32,128]{1,0:T(8,128)(2,1)}, u32[]{:S(2)}) copy-start(bf16[32,128]{1,0:T(8,128)(2,1)} %copy-done.13) | copy-start | bytes 24580
  35.8 10.7 %copy-start.11 = (bf16[512,2176]{1,0:T(8,128)(2,1)S(1)}, bf16[512,2176]{1,0:T(8,128)(2,1)}, u32[]{:S(2)}) copy-start(bf16[512,2176]{1,0:T(8,128)(2,1)} %get-tuple-element.39) | copy-start | bytes 6684676
  36.6 7.3 %collective-permute-start.20 = (bf16[32,2176]{1,0:T(8,128)(2,1)}, bf16[32,2176]{1,0:T(8,128)(2,1)S(1)}, u32[]{:S(2)}, u32[]{:S(2)}) collective-permute-start(bf16[32,2176]{1,0:T(8,128)(2,1)} %get-tuple-element.49), channel_id=1, source_target_pairs={{0,8},{2,10},{4,12},{6,14},{8,16},{10,18},{12,20},{14,22},{16,24},... | collective-permute-start | bytes 417800 | tf_op jit(solution)/shard_map/ppermute | solution.py:119
  36.8 29.8 %collective-permute-start.5 = (bf16[1024,384]{1,0:T(8,128)(2,1)S(1)}, bf16[1024,384]{1,0:T(8,128)(2,1)S(1)}, u32[]{:S(2)}, u32[]{:S(2)}) collective-permute-start(bf16[1024,384]{1,0:T(8,128)(2,1)S(1)} %bitcast.157), channel_id=1, source_target_pairs={{0,1},{1,0},{2,3},{3,2},{4,5},{5,4},{6,7},{7,6},{8,9},{9,8},{10,11... | collective-permute-start | bytes 2359304 | tf_op jit(solution)/shard_map/ppermute | solution.py:187
  38.4 35.8 %collective-permute-start.6 = (bf16[1024,384]{1,0:T(8,128)(2,1)}, bf16[1024,384]{1,0:T(8,128)(2,1)S(1)}, u32[]{:S(2)}, u32[]{:S(2)}) collective-permute-start(bf16[1024,384]{1,0:T(8,128)(2,1)} %bitcast.168), channel_id=1, source_target_pairs={{0,1},{1,0},{2,3},{3,2},{4,5},{5,4},{6,7},{7,6},{8,9},{9,8},{10,11... | collective-permute-start | bytes 2359304 | tf_op jit(solution)/shard_map/ppermute | solution.py:187
  39.9 18.0 %copy-start.12 = (bf16[512,2176]{1,0:T(8,128)(2,1)S(1)}, bf16[512,2176]{1,0:T(8,128)(2,1)}, u32[]{:S(2)}) copy-start(bf16[512,2176]{1,0:T(8,128)(2,1)} %get-tuple-element.48) | copy-start | bytes 6684676
  40.0 48.5 %collective-permute-start.12 = (bf16[384,1024]{1,0:T(8,128)(2,1)}, bf16[384,1024]{1,0:T(8,128)(2,1)S(1)}, u32[]{:S(2)}, u32[]{:S(2)}) collective-permute-start(bf16[384,1024]{1,0:T(8,128)(2,1)} %bitcast.12), channel_id=1, source_target_pairs={{0,1},{1,0},{2,3},{3,2},{4,5},{5,4},{6,7},{7,6},{8,9},{9,8},{10,11... | collective-permute-start | bytes 2359304 | tf_op jit(solution)/shard_map/ppermute | solution.py:187
  41.5 15.5 %collective-permute-start.3 = (bf16[128,2176]{1,0:T(8,128)(2,1)S(1)}, bf16[128,2176]{1,0:T(8,128)(2,1)S(1)}, u32[]{:S(2)}, u32[]{:S(2)}) collective-permute-start(bf16[128,2176]{1,0:T(8,128)(2,1)S(1)} %pad_maximum_fusion), channel_id=1, source_target_pairs={{0,4},{2,6},{4,0},{6,2},{8,12},{10,14},{12,8},{14,10},{16,20},{18,... | collective-permute-start | bytes 1671176 | tf_op jit(solution)/shard_map/ppermute | solution.py:114
  44.9 20.7 %collective-permute-start.21 = (bf16[128,2176]{1,0:T(8,128)(2,1)S(1)}, bf16[128,2176]{1,0:T(8,128)(2,1)S(1)}, u32[]{:S(2)}, u32[]{:S(2)}) collective-permute-start(bf16[128,2176]{1,0:T(8,128)(2,1)S(1)} %pad_maximum_fusion.1), channel_id=1, source_target_pairs={{0,4},{2,6},{4,0},{6,2},{8,12},{10,14},{12,8},{14,10},{16,20},{18,... | collective-permute-start | bytes 1671176 | tf_op jit(solution)/shard_map/ppermute | solution.py:114
  57.9 8.6 %collective-permute-start.4 = (bf16[256,2176]{1,0:T(8,128)(2,1)}, bf16[256,2176]{1,0:T(8,128)(2,1)S(1)}, u32[]{:S(2)}, u32[]{:S(2)}) collective-permute-start(bf16[256,2176]{1,0:T(8,128)(2,1)} %get-tuple-element.10), channel_id=1, source_target_pairs={{0,2},{2,0},{4,6},{6,4},{8,10},{10,8},{12,14},{14,12},{16,18},{18,... | collective-permute-start | bytes 3342344 | tf_op jit(solution)/shard_map/ppermute | solution.py:114
  66.5 9.1 %collective-permute-start.22 = (bf16[256,2176]{1,0:T(8,128)(2,1)}, bf16[256,2176]{1,0:T(8,128)(2,1)S(1)}, u32[]{:S(2)}, u32[]{:S(2)}) collective-permute-start(bf16[256,2176]{1,0:T(8,128)(2,1)} %get-tuple-element.12), channel_id=1, source_target_pairs={{0,2},{2,0},{4,6},{6,4},{8,10},{10,8},{12,14},{14,12},{16,18},{18,... | collective-permute-start | bytes 3342344 | tf_op jit(solution)/shard_map/ppermute | solution.py:114
  90.4 12.5 %collective-permute-start.13 = (f32[256,1024]{1,0:T(8,128)}, f32[256,1024]{1,0:T(8,128)}, u32[]{:S(2)}, u32[]{:S(2)}) collective-permute-start(f32[256,1024]{1,0:T(8,128)} %slice.223), channel_id=1, source_target_pairs={{0,2},{2,0},{4,6},{6,4},{8,10},{10,8},{12,14},{14,12},{16,18},{18,... | collective-permute-start | bytes 3145736 | tf_op jit(solution)/shard_map/ppermute | solution.py:114
  91.5 14.8 %collective-permute-start.7 = (f32[256,1024]{1,0:T(8,128)}, f32[256,1024]{1,0:T(8,128)}, u32[]{:S(2)}, u32[]{:S(2)}) collective-permute-start(f32[256,1024]{1,0:T(8,128)} %slice.215), channel_id=1, source_target_pairs={{0,2},{2,0},{4,6},{6,4},{8,10},{10,8},{12,14},{14,12},{16,18},{18,... | collective-permute-start | bytes 3145736 | tf_op jit(solution)/shard_map/ppermute | solution.py:114
  97.3 4.8 %copy-start.10 = (bf16[1,32,4096]{2,1,0:T(8,128)(2,1)S(1)}, bf16[1,32,4096]{2,1,0:T(8,128)(2,1)}, u32[]{:S(2)}) copy-start(bf16[1,32,4096]{2,1,0:T(8,128)(2,1)} %stack_reshape.6) | copy-start | bytes 786436
  97.3 11.0 %collective-permute-start.28 = (f32[256,1024]{1,0:T(8,128)}, f32[256,1024]{1,0:T(8,128)}, u32[]{:S(2)}, u32[]{:S(2)}) collective-permute-start(f32[256,1024]{1,0:T(8,128)} %slice.243), channel_id=1, source_target_pairs={{0,2},{2,0},{4,6},{6,4},{8,10},{10,8},{12,14},{14,12},{16,18},{18,... | collective-permute-start | bytes 3145736 | tf_op jit(solution)/shard_map/ppermute | solution.py:114
  101.6 9.6 %collective-permute-start.23 = (f32[256,1024]{1,0:T(8,128)}, f32[256,1024]{1,0:T(8,128)}, u32[]{:S(2)}, u32[]{:S(2)}) collective-permute-start(f32[256,1024]{1,0:T(8,128)} %slice.235), channel_id=1, source_target_pairs={{0,2},{2,0},{4,6},{6,4},{8,10},{10,8},{12,14},{14,12},{16,18},{18,... | collective-permute-start | bytes 3145736 | tf_op jit(solution)/shard_map/ppermute | solution.py:114
  104.7 3.6 %copy-start.5 = (f32[512,1024]{1,0:T(8,128)S(1)}, f32[512,1024]{1,0:T(8,128)}, u32[]{:S(2)}) copy-start(f32[512,1024]{1,0:T(8,128)} %copy-done.4) | copy-start | bytes 6291460
  104.7 14.9 %collective-permute-start.14 = (f32[128,1024]{1,0:T(8,128)S(1)}, f32[128,1024]{1,0:T(8,128)S(1)}, u32[]{:S(2)}, u32[]{:S(2)}) collective-permute-start(f32[128,1024]{1,0:T(8,128)S(1)} %slice.225), channel_id=1, source_target_pairs={{0,4},{2,6},{4,0},{6,2},{8,12},{10,14},{12,8},{14,10},{16,20},{18,... | collective-permute-start | bytes 1572872 | tf_op jit(solution)/shard_map/ppermute | solution.py:114
  107.7 3.6 %copy-start.2 = (f32[512,1024]{1,0:T(8,128)S(1)}, f32[512,1024]{1,0:T(8,128)}, u32[]{:S(2)}) copy-start(f32[512,1024]{1,0:T(8,128)} %copy-done.1) | copy-start | bytes 6291460
  107.7 23.1 %collective-permute-start.8 = (f32[128,1024]{1,0:T(8,128)S(1)}, f32[128,1024]{1,0:T(8,128)S(1)}, u32[]{:S(2)}, u32[]{:S(2)}) collective-permute-start(f32[128,1024]{1,0:T(8,128)S(1)} %slice.217), channel_id=1, source_target_pairs={{0,4},{2,6},{4,0},{6,2},{8,12},{10,14},{12,8},{14,10},{16,20},{18,... | collective-permute-start | bytes 1572872 | tf_op jit(solution)/shard_map/ppermute | solution.py:114
  109.7 32.3 %collective-permute-start.29 = (f32[128,1024]{1,0:T(8,128)S(1)}, f32[128,1024]{1,0:T(8,128)S(1)}, u32[]{:S(2)}, u32[]{:S(2)}) collective-permute-start(f32[128,1024]{1,0:T(8,128)S(1)} %slice.245), channel_id=1, source_target_pairs={{0,4},{2,6},{4,0},{6,2},{8,12},{10,14},{12,8},{14,10},{16,20},{18,... | collective-permute-start | bytes 1572872 | tf_op jit(solution)/shard_map/ppermute | solution.py:114
  112.7 39.6 %collective-permute-start.24 = (f32[128,1024]{1,0:T(8,128)S(1)}, f32[128,1024]{1,0:T(8,128)S(1)}, u32[]{:S(2)}, u32[]{:S(2)}) collective-permute-start(f32[128,1024]{1,0:T(8,128)S(1)} %slice.237), channel_id=1, source_target_pairs={{0,4},{2,6},{4,0},{6,2},{8,12},{10,14},{12,8},{14,10},{16,20},{18,... | collective-permute-start | bytes 1572872 | tf_op jit(solution)/shard_map/ppermute | solution.py:114
  119.6 34.9 %collective-permute-start.17 = (f32[32,1024]{1,0:T(8,128)S(1)}, f32[32,1024]{1,0:T(8,128)S(1)}, u32[]{:S(2)}, u32[]{:S(2)}) collective-permute-start(f32[32,1024]{1,0:T(8,128)S(1)} %get-tuple-element.20), channel_id=1, source_target_pairs={{0,24},{2,26},{4,28},{6,30},{8,0},{10,2},{12,4},{14,6},{16,8},{18,... | collective-permute-start | bytes 393224 | tf_op jit(solution)/shard_map/ppermute | solution.py:119
  123.1 33.4 %collective-permute-start.16 = (f32[32,1024]{1,0:T(8,128)S(1)}, f32[32,1024]{1,0:T(8,128)S(1)}, u32[]{:S(2)}, u32[]{:S(2)}) collective-permute-start(f32[32,1024]{1,0:T(8,128)S(1)} %get-tuple-element.21), channel_id=1, source_target_pairs={{0,16},{2,18},{4,20},{6,22},{8,24},{10,26},{12,28},{14,30},{16,0},... | collective-permute-start | bytes 393224 | tf_op jit(solution)/shard_map/ppermute | solution.py:119
  130.8 27.7 %collective-permute-start.15 = (f32[32,1024]{1,0:T(8,128)S(1)}, f32[32,1024]{1,0:T(8,128)S(1)}, u32[]{:S(2)}, u32[]{:S(2)}) collective-permute-start(f32[32,1024]{1,0:T(8,128)S(1)} %get-tuple-element.19), channel_id=1, source_target_pairs={{0,8},{2,10},{4,12},{6,14},{8,16},{10,18},{12,20},{14,22},{16,24},... | collective-permute-start | bytes 393224 | tf_op jit(solution)/shard_map/ppermute | solution.py:119
  142.0 16.5 %collective-permute-start.11 = (f32[32,1024]{1,0:T(8,128)S(1)}, f32[32,1024]{1,0:T(8,128)S(1)}, u32[]{:S(2)}, u32[]{:S(2)}) collective-permute-start(f32[32,1024]{1,0:T(8,128)S(1)} %get-tuple-element.17), channel_id=1, source_target_pairs={{0,24},{2,26},{4,28},{6,30},{8,0},{10,2},{12,4},{14,6},{16,8},{18,... | collective-permute-start | bytes 393224 | tf_op jit(solution)/shard_map/ppermute | solution.py:119
  152.3 14.4 %collective-permute-start.10 = (f32[32,1024]{1,0:T(8,128)S(1)}, f32[32,1024]{1,0:T(8,128)S(1)}, u32[]{:S(2)}, u32[]{:S(2)}) collective-permute-start(f32[32,1024]{1,0:T(8,128)S(1)} %get-tuple-element.18), channel_id=1, source_target_pairs={{0,16},{2,18},{4,20},{6,22},{8,24},{10,26},{12,28},{14,30},{16,0},... | collective-permute-start | bytes 393224 | tf_op jit(solution)/shard_map/ppermute | solution.py:119
  154.5 31.8 %copy-start.8 = (bf16[2,32,2048]{2,1,0:T(8,128)(2,1)S(1)}, bf16[2,32,2048]{2,1,0:T(8,128)(2,1)}, u32[]{:S(2)}) copy-start(bf16[2,32,2048]{2,1,0:T(8,128)(2,1)} %param.17) | copy-start | bytes 786436
  154.5 14.1 %collective-permute-start.9 = (f32[32,1024]{1,0:T(8,128)S(1)}, f32[32,1024]{1,0:T(8,128)S(1)}, u32[]{:S(2)}, u32[]{:S(2)}) collective-permute-start(f32[32,1024]{1,0:T(8,128)S(1)} %get-tuple-element.16), channel_id=1, source_target_pairs={{0,8},{2,10},{4,12},{6,14},{8,16},{10,18},{12,20},{14,22},{16,24},... | collective-permute-start | bytes 393224 | tf_op jit(solution)/shard_map/ppermute | solution.py:119
  156.5 16.6 %collective-permute-start.32 = (f32[32,1024]{1,0:T(8,128)S(1)}, f32[32,1024]{1,0:T(8,128)S(1)}, u32[]{:S(2)}, u32[]{:S(2)}) collective-permute-start(f32[32,1024]{1,0:T(8,128)S(1)} %get-tuple-element.26), channel_id=1, source_target_pairs={{0,24},{2,26},{4,28},{6,30},{8,0},{10,2},{12,4},{14,6},{16,8},{18,... | collective-permute-start | bytes 393224 | tf_op jit(solution)/shard_map/ppermute | solution.py:119
  158.4 23.5 %collective-permute-start.31 = (f32[32,1024]{1,0:T(8,128)S(1)}, f32[32,1024]{1,0:T(8,128)S(1)}, u32[]{:S(2)}, u32[]{:S(2)}) collective-permute-start(f32[32,1024]{1,0:T(8,128)S(1)} %get-tuple-element.27), channel_id=1, source_target_pairs={{0,16},{2,18},{4,20},{6,22},{8,24},{10,26},{12,28},{14,30},{16,0},... | collective-permute-start | bytes 393224 | tf_op jit(solution)/shard_map/ppermute | solution.py:119
  158.5 23.5 %collective-permute-start.30 = (f32[32,1024]{1,0:T(8,128)S(1)}, f32[32,1024]{1,0:T(8,128)S(1)}, u32[]{:S(2)}, u32[]{:S(2)}) collective-permute-start(f32[32,1024]{1,0:T(8,128)S(1)} %get-tuple-element.25), channel_id=1, source_target_pairs={{0,8},{2,10},{4,12},{6,14},{8,16},{10,18},{12,20},{14,22},{16,24},... | collective-permute-start | bytes 393224 | tf_op jit(solution)/shard_map/ppermute | solution.py:119
  166.7 15.3 %collective-permute-start.27 = (f32[32,1024]{1,0:T(8,128)S(1)}, f32[32,1024]{1,0:T(8,128)S(1)}, u32[]{:S(2)}, u32[]{:S(2)}) collective-permute-start(f32[32,1024]{1,0:T(8,128)S(1)} %get-tuple-element.23), channel_id=1, source_target_pairs={{0,24},{2,26},{4,28},{6,30},{8,0},{10,2},{12,4},{14,6},{16,8},{18,... | collective-permute-start | bytes 393224 | tf_op jit(solution)/shard_map/ppermute | solution.py:119
  168.7 17.5 %collective-permute-start.26 = (f32[32,1024]{1,0:T(8,128)S(1)}, f32[32,1024]{1,0:T(8,128)S(1)}, u32[]{:S(2)}, u32[]{:S(2)}) collective-permute-start(f32[32,1024]{1,0:T(8,128)S(1)} %get-tuple-element.24), channel_id=1, source_target_pairs={{0,16},{2,18},{4,20},{6,22},{8,24},{10,26},{12,28},{14,30},{16,0},... | collective-permute-start | bytes 393224 | tf_op jit(solution)/shard_map/ppermute | solution.py:119
  173.2 13.1 %collective-permute-start.25 = (f32[32,1024]{1,0:T(8,128)S(1)}, f32[32,1024]{1,0:T(8,128)S(1)}, u32[]{:S(2)}, u32[]{:S(2)}) collective-permute-start(f32[32,1024]{1,0:T(8,128)S(1)} %get-tuple-element.22), channel_id=1, source_target_pairs={{0,8},{2,10},{4,12},{6,14},{8,16},{10,18},{12,20},{14,22},{16,24},... | collective-permute-start | bytes 393224 | tf_op jit(solution)/shard_map/ppermute | solution.py:119
  (11 other events, 21.1 us)

commit v2 on v1

v2 whole, which is shorter than its diff:
```python
import functools
import math

import jax
import jax.numpy as jnp
from jax import lax
from jax.experimental import pallas as pl
from jax.experimental.pallas import tpu as pltpu
from jax.sharding import PartitionSpec as P

HEADS = 32
KV_HEADS = 4
HEAD = 128
TOP = 8
CAP = 3
LANES = 128
OUTER = 4
OUT_COLUMNS = 512
RADIX = 64
STEP_BYTES = 1 << 22

norm_epsilon = 1e-06


def attend(query_rows, key_cache, value_cache, new_keys, new_values, cache_lengths, step_index):
    rows_here = query_rows.shape[0]
    cache_len = key_cache.shape[1]
    steps_all = new_keys.shape[0]
    grouped = query_rows.reshape(rows_here, KV_HEADS, HEADS // KV_HEADS, HEAD)
    keys_cached = key_cache.reshape(rows_here, cache_len, KV_HEADS, HEAD)
    values_cached = value_cache.reshape(rows_here, cache_len, KV_HEADS, HEAD)
    keys_fresh = new_keys.reshape(steps_all, rows_here, KV_HEADS, HEAD)
    values_fresh = new_values.reshape(steps_all, rows_here, KV_HEADS, HEAD)
    score_scale = 1.0 / math.sqrt(HEAD)
    cache_scores = (
        jnp.einsum("rkgh,rckh->rkgc", grouped, keys_cached, preferred_element_type=jnp.float32)
        * score_scale
    )
    fresh_scores = (
        jnp.einsum("rkgh,srkh->rkgs", grouped, keys_fresh, preferred_element_type=jnp.float32)
        * score_scale
    )
    cache_mask = (jnp.arange(cache_len, dtype=jnp.int32)[None, :] < cache_lengths[:, None])[
        :, None, None, :
    ]
    fresh_mask = (jnp.arange(steps_all, dtype=jnp.int32) <= step_index)[None, None, None, :]
    row_max = jnp.maximum(
        jnp.max(jnp.where(cache_mask, cache_scores, -1e30), axis=-1),
        jnp.max(jnp.where(fresh_mask, fresh_scores, -1e30), axis=-1),
    )
    cache_exp = jnp.where(cache_mask, jnp.exp(cache_scores - row_max[..., None]), 0.0)
    fresh_exp = jnp.where(fresh_mask, jnp.exp(fresh_scores - row_max[..., None]), 0.0)
    row_total = jnp.sum(cache_exp, axis=-1) + jnp.sum(fresh_exp, axis=-1)
    cache_probs = (cache_exp / row_total[..., None]).astype(jnp.bfloat16)
    fresh_probs = (fresh_exp / row_total[..., None]).astype(jnp.bfloat16)
    summed = jnp.einsum(
        "rkgc,rckh->rkgh", cache_probs, values_cached, preferred_element_type=jnp.float32
    )
    summed = summed + jnp.einsum(
        "rkgs,srkh->rkgh", fresh_probs, values_fresh, preferred_element_type=jnp.float32
    )
    return summed.astype(jnp.bfloat16).reshape(rows_here, HEADS * HEAD)


VMEM = pl.BlockSpec(memory_space=pltpu.VMEM)
SMEM = pl.BlockSpec(memory_space=pltpu.SMEM)


def exact_dot(left, right):
    return jnp.dot(
        left.astype(jnp.bfloat16), right.astype(jnp.bfloat16), preferred_element_type=jnp.float32
    )


def prepare_kernel(
    column_ref,
    hot_ref,
    trainer_ref,
    replica_hot_ref,
    gain_ref,
    hidden_ref,
    weights_ref,
    routes_ref,
    picks_ref,
    *packed_refs,
    dp_count,
):
    tokens = hidden_ref.shape[1]
    width = hidden_ref.shape[2]
    block = width // dp_count
    devices = trainer_ref.shape[1]
    entries = tokens * TOP
    trainer = trainer_ref[...]
    replica_hot = replica_hot_ref[...]
    hosted = jnp.zeros_like(replica_hot)
    for h in range(hot_ref.shape[0]):
        hosted = jnp.where(replica_hot == h, hot_ref[h], hosted)
    trainer = trainer.astype(jnp.float32)
    hosted = hosted.astype(jnp.float32)
    entry_row = lax.broadcasted_iota(jnp.int32, (entries, 1), 0)
    token_map = (
        lax.broadcasted_iota(jnp.int32, (entries, tokens), 1) == entry_row // TOP
    ).astype(jnp.float32)
    turn_map = (
        lax.broadcasted_iota(jnp.int32, (entries, TOP), 1) == entry_row % TOP
    ).astype(jnp.float32)
    earlier = (
        lax.broadcasted_iota(jnp.int32, (entries, entries), 1) <= entry_row
    ).astype(jnp.float32)
    ordered = (
        lax.broadcasted_iota(jnp.int32, (devices, devices), 0)
        <= lax.broadcasted_iota(jnp.int32, (devices, devices), 1)
    ).astype(jnp.float32)

    def as_column(table):
        return jnp.sum(exact_dot(token_map, table) * turn_map, axis=1, keepdims=True)

    gain = gain_ref[...].astype(jnp.float32)
    for step_index, packed_ref in enumerate(packed_refs):
        for s in range(dp_count):
            start = lax.rem(column_ref[0] + s, dp_count) * block
            if s == 0:
                values = hidden_ref[step_index].astype(jnp.float32)
                mean_square = jnp.mean(values * values, axis=-1, keepdims=True)
                scale = lax.rsqrt(mean_square + norm_epsilon)
            columns = pl.ds(pl.multiple_of(start, LANES), block)
            part = hidden_ref[step_index, :, columns].astype(jnp.float32)
            part = part * scale * gain_ref[:, columns].astype(jnp.float32)
            packed_ref[:, s * block : (s + 1) * block] = part.astype(jnp.bfloat16)
        top_weights = weights_ref[step_index]
        gates = (top_weights / jnp.sum(top_weights, axis=-1, keepdims=True)).astype(jnp.bfloat16)
        picks = picks_ref[step_index]
        pick_high = picks // RADIX
        pick_low = picks - pick_high * RADIX
        chosen = as_column(routes_ref[step_index].astype(jnp.float32))
        pick = as_column(pick_high.astype(jnp.float32)) * RADIX + as_column(
            pick_low.astype(jnp.float32)
        )
        gate = as_column(gates.astype(jnp.float32))
        at_home = (trainer == chosen).astype(jnp.float32)
        at_replica = (hosted == chosen).astype(jnp.float32)
        copies = 1.0 + jnp.sum(at_replica, axis=1, keepdims=True)
        order = exact_dot(at_replica, ordered) * at_replica
        replica_index = pick - copies * jnp.floor((pick + 0.5) / copies)
        first = (replica_index == 0.0).astype(jnp.float32)
        home_slot = at_home * first
        replica_slot = (order == replica_index).astype(jnp.float32) * (1.0 - first)
        home_rank = jnp.sum(
            exact_dot(earlier, home_slot) * home_slot, axis=1, keepdims=True
        )
        replica_rank = jnp.sum(
            exact_dot(earlier, replica_slot) * replica_slot, axis=1, keepdims=True
        )
        kept = jnp.where(home_rank + replica_rank <= CAP, gate, 0.0) * at_home
        spread = lax.dot_general(
            token_map.astype(jnp.bfloat16),
            kept.astype(jnp.bfloat16),
            (((0,), (0,)), ((), ())),
            preferred_element_type=jnp.float32,
        )
        packed_ref[:, width:] = jnp.zeros((tokens, packed_ref.shape[1] - width), jnp.bfloat16)
        packed_ref[:, width : width + devices] = spread.astype(jnp.bfloat16)


def join_kernel(*refs):
    out_ref = refs[-1]
    row = 0
    for ref in refs[:-1]:
        out_ref[row : row + ref.shape[0], :] = ref[...]
        row += ref.shape[0]


def join(parts):
    rows = sum(part.shape[0] for part in parts)
    return pl.pallas_call(
        join_kernel,
        out_shape=jax.ShapeDtypeStruct((rows, parts[0].shape[1]), parts[0].dtype),
        in_specs=[VMEM] * len(parts),
        out_specs=VMEM,
    )(*parts)


def own_gate(packed_gates, device):
    lane = lax.broadcasted_iota(jnp.int32, packed_gates.shape, 1)
    return jnp.sum(
        jnp.where(lane == device, packed_gates.astype(jnp.float32), 0.0), axis=1, keepdims=True
    )


def weighted_out(units, gate, down_ref):
    expert_out = jnp.dot(units, down_ref[...], preferred_element_type=jnp.float32)
    return gate * expert_out.astype(jnp.bfloat16).astype(jnp.float32)


def units_kernel(
    device_ref,
    here_ref,
    there_ref,
    gate_own_ref,
    gate_rest_ref,
    up_own_ref,
    up_rest_ref,
    down_ref,
    units_here_ref,
    units_there_ref,
    out_here_ref,
    out_there_ref,
    *,
    width,
):
    block = gate_own_ref.shape[0]

    def project(rows_ref, own_ref, rest_ref):
        return jnp.dot(
            rows_ref[:, :block], own_ref[...], preferred_element_type=jnp.float32
        ) + jnp.dot(rows_ref[:, block:width], rest_ref[...], preferred_element_type=jnp.float32)

    for rows_ref, units_ref, out_ref in (
        (there_ref, units_there_ref, out_there_ref),
        (here_ref, units_here_ref, out_here_ref),
    ):
        gate_part = project(rows_ref, gate_own_ref, gate_rest_ref)
        up_part = project(rows_ref, up_own_ref, up_rest_ref)
        units = (gate_part / (1.0 + jnp.exp(-gate_part)) * up_part).astype(jnp.bfloat16)
        units_ref[...] = units
        out_ref[...] = weighted_out(units, own_gate(rows_ref[:, width:], device_ref[0]), down_ref)


def out_kernel(
    device_ref,
    here_ref,
    there_ref,
    units_here_ref,
    units_there_ref,
    down_ref,
    out_here_ref,
    out_there_ref,
):
    for rows_ref, units_ref, out_ref in (
        (there_ref, units_there_ref, out_there_ref),
        (here_ref, units_here_ref, out_here_ref),
    ):
        out_ref[...] = weighted_out(
            units_ref[...], own_gate(rows_ref[...], device_ref[0]), down_ref
        )


def roll_blocks(rows, start, count):
    width = rows.shape[1] // count
    twice = jnp.concatenate([rows, rows], axis=1)
    return lax.dynamic_slice_in_dim(twice, start * width, rows.shape[1], axis=1)


def swap(value, axis_size, stride):
    return lax.ppermute(value, "ep", [(i, i ^ stride) for i in range(axis_size)])


def pull(value, axis_size, inner, offset):
    outer = axis_size // inner
    return lax.ppermute(
        value,
        "ep",
        [
            (z * inner + r, (z - offset) % outer * inner + r)
            for z in range(outer)
            for r in range(inner)
        ],
    )


def middle_strides(inner):
    stride = inner // 2
    while stride > 1:
        yield stride
        stride //= 2


def gather_rows(rows, axis_size, inner, inner_first):
    outer = axis_size // inner
    count = rows.shape[0]
    held = rows
    if not inner_first:
        pulled = [pull(held, axis_size, inner, r) for r in range(1, outer)]
        held = join([held] + pulled)
    for stride in middle_strides(inner):
        held = join([held, swap(held, axis_size, stride)])
    if inner_first:
        pulled = [held] + [pull(held, axis_size, inner, r) for r in range(1, outer)]
        held = join(
            [part[row : row + count] for row in range(0, held.shape[0], count) for part in pulled]
        )
    return held, swap(held, axis_size, 1)


def scatter_sum(keep, send, axis_size, inner):
    outer = axis_size // inner
    got = swap(send, axis_size, 1)
    for stride in reversed(list(middle_strides(inner))):
        half = keep.shape[0] // 2
        send = keep[half:] + got[half:]
        keep = keep[:half] + got[:half]
        got = swap(send, axis_size, stride)
    rows = keep.shape[0] // outer
    pulled = [
        pull(
            keep[r * rows : (r + 1) * rows] + got[r * rows : (r + 1) * rows],
            axis_size,
            inner,
            outer - r,
        )
        for r in range(1, outer)
    ]
    total = keep[:rows] + got[:rows]
    for part in pulled:
        total = total + part
    return total


def one_step_at_a_time(hidden):
    return lax.axis_size("ep") * hidden.shape[1] * hidden.shape[2] * 2 > STEP_BYTES


def compute(
    hidden,
    norm_gain,
    gate_weights,
    routes,
    replica_pick,
    trainer_experts,
    hot_experts,
    replica_hot,
    w_gate,
    w_up,
    w_down,
    queries,
    key_cache,
    value_cache,
    new_keys,
    new_values,
    cache_lengths,
):
    ep_count = lax.axis_size("ep")
    dp_count = lax.axis_size("dp")
    my_device = lax.axis_index("ep")
    my_column = lax.axis_index("dp")
    inner = max(1, ep_count // OUTER)
    steps, tokens_here, width = hidden.shape
    block = width // dp_count

    def complete(shard):
        return [shard] + [
            lax.ppermute(shard, "dp", [(i, (i - s) % dp_count) for i in range(dp_count)])
            for s in range(1, dp_count)
        ]

    gate_parts = complete(w_gate[0])
    up_parts = complete(w_up[0])
    down_parts = complete(w_down[0])

    lanes = -(-ep_count // LANES) * LANES
    packed_shape = jax.ShapeDtypeStruct((tokens_here, width + lanes), jnp.bfloat16)
    packed = pl.pallas_call(
        functools.partial(prepare_kernel, dp_count=dp_count),
        out_shape=[packed_shape] * steps,
        in_specs=[SMEM, SMEM] + [VMEM] * 7,
        out_specs=[VMEM] * steps,
    )(
        my_column.reshape(1),
        hot_experts,
        trainer_experts.reshape(1, ep_count),
        replica_hot.reshape(1, ep_count),
        norm_gain.reshape(1, width),
        hidden,
        gate_weights,
        routes,
        replica_pick,
    )
    gate_rest = jnp.concatenate(gate_parts[1:])
    up_rest = jnp.concatenate(up_parts[1:])
    one_by_one = one_step_at_a_time(hidden)
    span = max(1, OUT_COLUMNS // block)
    down_groups = [down_parts[0]] + [
        jnp.concatenate(down_parts[s : s + span], axis=1) for s in range(1, dp_count, span)
    ]
    device = my_device.reshape(1)

    def process(rows, inner_first):
        here, there = gather_rows(rows, ep_count, inner, inner_first)
        count = here.shape[0]
        hidden_units = w_gate.shape[2]

        def partial_sums(columns):
            return [jax.ShapeDtypeStruct((count, columns), jnp.float32)] * 2

        units_here, units_there, keep, send = pl.pallas_call(
            functools.partial(units_kernel, width=width),
            out_shape=[jax.ShapeDtypeStruct((count, hidden_units), jnp.bfloat16)] * 2
            + partial_sums(block),
            in_specs=[SMEM] + [VMEM] * 7,
            out_specs=[VMEM] * 4,
        )(
            device,
            here,
            there,
            gate_parts[0],
            gate_rest,
            up_parts[0],
            up_rest,
            down_groups[0],
        )
        gate_lanes = pl.BlockSpec((count, lanes), lambda i: (0, width // lanes))
        blocks = []
        for s, down_part in enumerate(down_groups):
            columns = down_part.shape[1]
            if s:
                if one_by_one:
                    units_here, _ = lax.optimization_barrier((units_here, blocks[-1]))
                keep, send = pl.pallas_call(
                    out_kernel,
                    grid=(1,),
                    out_shape=partial_sums(columns),
                    in_specs=[
                        SMEM,
                        gate_lanes,
                        gate_lanes,
                        pl.BlockSpec((count, hidden_units), lambda i: (0, 0)),
                        pl.BlockSpec((count, hidden_units), lambda i: (0, 0)),
                        pl.BlockSpec((hidden_units, columns), lambda i: (0, 0)),
                    ],
                    out_specs=[pl.BlockSpec((count, columns), lambda i: (0, 0))] * 2,
                )(device, here, there, units_here, units_there, down_part)
            blocks.append(scatter_sum(keep, send, ep_count, inner))
        return jnp.concatenate(blocks, axis=1)

    if one_by_one:
        sums = lax.map(lambda rows: process(rows, False), jnp.stack(packed))
    else:
        sums = [process(rows, step_index > 0) for step_index, rows in enumerate(packed)]

    context_steps = [
        attend(
            queries[step_index],
            key_cache,
            value_cache,
            new_keys,
            new_values,
            cache_lengths,
            step_index,
        )
        for step_index in range(steps)
    ]

    mixed_steps = []
    for step_index in range(steps):
        total = roll_blocks(sums[step_index], (dp_count - my_column) % dp_count, dp_count)
        mixed_steps.append(
            (hidden[step_index].astype(jnp.float32) + total).astype(jnp.bfloat16)
        )
    return (jnp.stack(mixed_steps), jnp.stack(context_steps))


def solution(mesh):
    return jax.shard_map(
        compute,
        mesh=mesh,
        in_specs=(
            P(None, ("ep", "dp"), None),
            P(),
            P(None, ("ep", "dp"), None),
            P(None, ("ep", "dp"), None),
            P(None, ("ep", "dp"), None),
            P(),
            P(),
            P(),
            P("ep", "dp", None),
            P("ep", "dp", None),
            P("ep", None, "dp"),
            P(None, ("ep", "dp"), None),
            P(("ep", "dp"), None, None),
            P(("ep", "dp"), None, None),
            P(None, ("ep", "dp"), None),
            P(None, ("ep", "dp"), None),
            P(("ep", "dp")),
        ),
        out_specs=(P(None, ("ep", "dp"), None), P(None, ("ep", "dp"), None)),
        check_vma=False,
    )
```

time: 188 us -> 172 us (0.915)
  Pallas kernels: 0 us -> 31.9 us
  waiting for transfers between devices: 74 us -> 45.3 us
  other arithmetic: 22 us -> 12 us
  local copies, waits for them, and re-layouts: 23.5 us -> 16.5 us
  matrix products: 18.3 us -> 12.4 us
  starting transfers between devices: 47.9 us -> 51.6 us
    pallas_call x0 -> x9, Pallas kernels: none -> 31.9 us  [the longest x2 13.7 us: process(): pl.pallas_call(functools.partial(units_kernel, width=width), out_shape=[j...]
    ppermute x12, waiting for transfers between devices: 39.7 us -> 17.7 us  [swap(): lax.ppermute(value, 'ep', [(i, i ^ stride) for i in range(axis_size)])]
    ppermute x3, waiting for transfers between devices: 15.9 us -> 0.01 us  [complete(): lax.ppermute(shard, 'dp', [(i, (i - s) % dp_count) for i in range(dp_coun...]
    dot_general x18 -> x0, matrix products: 12.6 us -> none  [the longest x4 5.15 us: process(): jnp.dot(units, down_part, preferred_element_type=jnp.float32)]
    ppermute x18, waiting for transfers between devices: 18.4 us -> 27.6 us  [pull(): lax.ppermute(value, 'ep', [(z * inner + r, (z - offset) % outer * inner +...]
    ppermute x18, starting transfers between devices: 35.8 us -> 41.2 us  [pull(): lax.ppermute(value, 'ep', [(z * inner + r, (z - offset) % outer * inner +...]
    reduce_sum x11 -> x0, other arithmetic: 4.63 us -> none  [the longest x1 1.13 us: scaled_norm(): mean_square = jnp.mean(values * values, axis=-1, keepdims=True)]
    unnamed x65 -> x60, local copies, waits for them, and re-layouts: 11.9 us -> 8.8 us
  transfers between devices with their start and end apart: 33 -> 33, of which waited for: 12 -> 13; matrix products, arithmetic and copies ran while one was open for 25% -> 18% of each run, Pallas kernels for 0% -> 17%
where the time goes in v2:
time: 172 us; the launch traced here: 171 us
  starting transfers between devices  51.6 us (30%)
  waiting for transfers between devices  45.3 us (26%)
  Pallas kernels  31.9 us (19%)
  local copies, waits for them, and re-layouts  16.5 us (10%)
  matrix products  12.4 us (7%)
  other arithmetic  12 us (7%)
    ppermute x18, starting transfers between devices, pull(): lax.ppermute(value, 'ep', [(z * inner + r, (z - offset) % outer * inner +...  41.2 us
    ppermute x18, waiting for transfers between devices, pull(): lax.ppermute(value, 'ep', [(z * inner + r, (z - offset) % outer * inner +...  27.6 us
    ppermute x12, waiting for transfers between devices, swap(): lax.ppermute(value, 'ep', [(i, i ^ stride) for i in range(axis_size)])  17.7 us
    pallas_call x2, Pallas kernels, process(): pl.pallas_call(functools.partial(units_kernel, width=width), out_shape=[j...  13.7 us
    unnamed x60, local copies, waits for them, and re-layouts  8.8 us
    pallas_call x4, Pallas kernels, join(): pl.pallas_call(join_kernel, out_shape=jax.ShapeDtypeStruct((rows, parts[0...  8.5 us
    ppermute x12, starting transfers between devices, swap(): lax.ppermute(value, 'ep', [(i, i ^ stride) for i in range(axis_size)])  6.84 us
    pallas_call x2, Pallas kernels, process(): pl.pallas_call(out_kernel, grid=(1,), out_shape=partial_sums(columns), in...  6.51 us
  transfers between devices with their start and end apart: 33, of which 13 were waited for; matrix products, arithmetic and copies ran while one was open for 18% of the time, Pallas kernels for 17%

profile of v2, /device:TPU:0, one launch (start us, length us, event | category | flops | bytes accessed | tf_op | source)
XLA Modules:
  0.0 170.7 jit_solution(3342765188011305017)
XLA Ops:
  0.7 1.5 copy.19.weights_ref
  2.2 1.4 copy.20.routes_ref
  3.6 1.4 copy.21.picks_ref
  4.9 1.3 reshape.88.gain_ref
  6.2 3.1 %shard_map.176 = (bf16[32,2176]{1,0:T(8,128)(2,1)}, bf16[32,2176]{1,0:T(8,128)(2,1)}) custom-call(s32[1]{0:T(128)} %bitcast.2.column_ref, s32[3]{0:T(128)} %hot_ref.1, s32[1,16]{1,0:T(1,128)} %bitcast.74, s32[1,16]{1,0:T(1,128)} %bitcast.75, bf16[1,2048]{1,0:T(2,128)(2,1)} %reshape.88.gain_ref, bf16[2,32,2048]{2,1,0:T(8,128)(2,1)} %hidden_ref.1, ...), custom_call_target="tpu_custom_call" | custom-call | tf_op jit(solution)/shard_map/pallas_call | solution.py:362
  9.4 5.1 %collective-permute-start = (bf16[32,2176]{1,0:T(8,128)(2,1)}, bf16[32,2176]{1,0:T(8,128)(2,1)S(1)}, u32[]{:S(2)}, u32[]{:S(2)}) collective-permute-start(bf16[32,2176]{1,0:T(8,128)(2,1)} %get-tuple-element.16.refs_0_), channel_id=1, source_target_pairs={{0,24},{2,26},{4,28},{6,30},{8,0},{10,2},{12,4},{14,6},{16,8},{18,... | collective-permute-start | bytes 417800 | tf_op jit(solution)/shard_map/ppermute | solution.py:260
  15.5 1.5 collective-permute-start.18
  17.0 1.5 collective-permute-start.5
  21.1 1.5 select_reduce_fusion.1
  24.4 1.7 shard_map.181
  26.1 2.5 %collective-permute-start.21 = (bf16[64,2176]{1,0:T(8,128)(2,1)}, bf16[64,2176]{1,0:T(8,128)(2,1)S(1)}, u32[]{:S(2)}, u32[]{:S(2)}) collective-permute-start(bf16[64,2176]{1,0:T(8,128)(2,1)} %shard_map.181), channel_id=1, source_target_pairs={{0,8},{2,10},{4,12},{6,14},{8,16},{10,18},{12,20},{14,22},{16,24},... | collective-permute-start | bytes 835592 | tf_op jit(solution)/shard_map/ppermute | solution.py:260
  28.5 1.7 %fusion.59 = (bf16[32,2176]{1,0:T(8,128)(2,1)}, bf16[32,2176]{1,0:T(8,128)(2,1)}) fusion(bf16[64,2176]{1,0:T(8,128)(2,1)} %shard_map.181), kind=kLoop, calls=%fused_computation.116 | loop fusion | bytes 557056 | tf_op jit(solution)/shard_map/slice | solution.py:290
  30.8 1.5 collective-permute-start.12
  33.2 2.0 %shard_map.177.refs_0_ = bf16[128,2176]{1,0:T(8,128)(2,1)} custom-call(bf16[32,2176]{1,0:T(8,128)(2,1)} %get-tuple-element.16.refs_0_, bf16[32,2176]{1,0:T(8,128)(2,1)} %copy-done.16, bf16[32,2176]{1,0:T(8,128)(2,1)} %copy-done.17, bf16[32,2176]{1,0:T(8,128)(2,1)} %copy-done.18), custom_call_target="tpu_custom_call" | custom-call | tf_op jit(solution)/shard_map/pallas_call | solution.py:175
  35.2 1.6 collective-permute-done.21
  37.8 9.3 %collective-permute-done.20 = bf16[64,2176]{1,0:T(8,128)(2,1)S(1)} collective-permute-done((bf16[64,2176]{1,0:T(8,128)(2,1)}, bf16[64,2176]{1,0:T(8,128)(2,1)S(1)}, u32[]{:S(2)}, u32[]{:S(2)}) %collective-permute-start.20) | collective-permute-done | bytes 278560 | tf_op jit(solution)/shard_map/ppermute | solution.py:260
  49.5 2.5 %shard_map.182.here_ref = bf16[256,2176]{1,0:T(8,128)(2,1)} custom-call(bf16[32,2176]{1,0:T(8,128)(2,1)} %get-tuple-element.61.refs_0_, bf16[32,2176]{1,0:T(8,128)(2,1)} %get-tuple-element.59.refs_1_, bf16[32,2176]{1,0:T(8,128)(2,1)} %get-tuple-element.57.refs_2_, bf16[32,2176]{1,0:T(8,128)(2,1)} %get-tuple-element.55.refs_3_, ...), custom_call_target="tpu_custom_call" | custom-call | tf_op jit(solution)/shard_map/pallas_call | solution.py:175
  52.0 3.2 %fusion.10 = (f32[32,4,8]{2,1,0:T(4,128)}, f32[32,4,8]{2,1,0:T(4,128)}, f32[32,4,8,32]{3,2,1,0:T(8,128)}) fusion(f32[32,4,8,32]{3,2,1,0:T(8,128)} %get-tuple-element.65, f32[32,4,8]{2,1,0:T(4,128)S(1)} %max.14, pred[32,32]{1,0:T(8,128)(4,1)S(1)} %iota_compare_fusion, bf16[32,4,8,128]{3,2,1,0:T(8,128)(2,1)S(1)} %bitcast.72, ...), kind=kOutput, calls=%fused_computation.39 | convolution fusion | flops 8583168 | bytes 1586176 | tf_op jit(solution)/shard_map/rkgh,rckh->rkgc/dot_general | solution.py:36
  55.2 6.7 %collective-permute-done.3.refs_1_ = bf16[128,2176]{1,0:T(8,128)(2,1)} collective-permute-done((bf16[128,2176]{1,0:T(8,128)(2,1)}, bf16[128,2176]{1,0:T(8,128)(2,1)}, u32[]{:S(2)}, u32[]{:S(2)}) %collective-permute-start.3) | collective-permute-done | bytes 557088 | tf_op jit(solution)/shard_map/ppermute | solution.py:255
  61.9 2.3 %shard_map.178.here_ref = bf16[256,2176]{1,0:T(8,128)(2,1)} custom-call(bf16[128,2176]{1,0:T(8,128)(2,1)} %shard_map.177.refs_0_, bf16[128,2176]{1,0:T(8,128)(2,1)} %collective-permute-done.3.refs_1_), custom_call_target="tpu_custom_call" | custom-call | tf_op jit(solution)/shard_map/pallas_call | solution.py:175
  64.3 1.2 select_reduce_fusion.2
  68.8 1.4 fusion.44
  72.4 6.8 %shard_map.183 = (bf16[256,384]{1,0:T(8,128)(2,1)}, bf16[256,384]{1,0:T(8,128)(2,1)}, f32[256,1024]{1,0:T(8,128)}, f32[256,1024]{1,0:T(8,128)}) custom-call(s32[1]{0:T(128)} %bitcast.1.device_ref, bf16[256,2176]{1,0:T(8,128)(2,1)} %shard_map.182.here_ref, bf16[256,2176]{1,0:T(8,128)(2,1)} %copy-done.2, bf16[1024,384]{1,0:T(8,128)(2,1)} %bitcast.68, ...), custom_call_target="tpu_custom_call" | custom-call | tf_op jit(solution)/shard_map/pallas_call | solution.py:395
  79.7 1.4 fusion.11
  81.2 3.2 %shard_map.184 = (f32[256,1024]{1,0:T(8,128)}, f32[256,1024]{1,0:T(8,128)}) custom-call(s32[1]{0:T(128)} %bitcast.1.device_ref, bf16[256,2176]{1,0:T(8,128)(2,1)} %shard_map.182.here_ref, bf16[256,2176]{1,0:T(8,128)(2,1)} %copy-done.2, bf16[256,384]{1,0:T(8,128)(2,1)} %get-tuple-element.26.units_here_ref, ...), custom_call_target="tpu_custom_call" | custom-call | tf_op jit(solution)/shard_map/pallas_call | solution.py:418
  84.5 1.2 fusion.45
  86.8 6.9 %shard_map.179 = (bf16[256,384]{1,0:T(8,128)(2,1)}, bf16[256,384]{1,0:T(8,128)(2,1)}, f32[256,1024]{1,0:T(8,128)}, f32[256,1024]{1,0:T(8,128)}) custom-call(s32[1]{0:T(128)} %bitcast.1.device_ref, bf16[256,2176]{1,0:T(8,128)(2,1)} %shard_map.178.here_ref, bf16[256,2176]{1,0:T(8,128)(2,1)} %copy-done.1, bf16[1024,384]{1,0:T(8,128)(2,1)} %bitcast.69, ...), custom_call_target="tpu_custom_call" | custom-call | tf_op jit(solution)/shard_map/pallas_call | solution.py:395
  94.2 1.7 fusion.1
  96.8 3.3 %shard_map.180 = (f32[256,1024]{1,0:T(8,128)}, f32[256,1024]{1,0:T(8,128)}) custom-call(s32[1]{0:T(128)} %bitcast.1.device_ref, bf16[256,2176]{1,0:T(8,128)(2,1)} %shard_map.178.here_ref, bf16[256,2176]{1,0:T(8,128)(2,1)} %copy-done.1, bf16[256,384]{1,0:T(8,128)(2,1)} %get-tuple-element.19.units_here_ref, ...), custom_call_target="tpu_custom_call" | custom-call | tf_op jit(solution)/shard_map/pallas_call | solution.py:418
  100.1 1.9 %pad_maximum_fusion = bf16[2,32,4096]{2,1,0:T(8,128)(2,1)} fusion(bf16[1,32,4096]{2,1,0:T(8,128)(2,1)} %stack_reshape.7, bf16[1,32,4096]{2,1,0:T(8,128)(2,1)S(1)} %stack_reshape.6), kind=kLoop, calls=%fused_computation.32 | loop fusion | flops 262144 | bytes 1048576 | tf_op jit(solution)/shard_map/stack | solution.py:459
  103.2 1.4 slice_add_fusion.1
  105.8 1.4 slice_add_fusion.7
  108.2 1.3 slice_add_fusion.5
  110.7 6.3 %collective-permute-done.24 = f32[128,1024]{1,0:T(8,128)S(1)} collective-permute-done((f32[128,1024]{1,0:T(8,128)S(1)}, f32[128,1024]{1,0:T(8,128)S(1)}, u32[]{:S(2)}, u32[]{:S(2)}) %collective-permute-start.24) | collective-permute-done | bytes 524320 | tf_op jit(solution)/shard_map/ppermute | solution.py:255
  117.1 3.3 %collective-permute-start.25 = (f32[32,1024]{1,0:T(8,128)S(1)}, f32[32,1024]{1,0:T(8,128)S(1)}, u32[]{:S(2)}, u32[]{:S(2)}) collective-permute-start(f32[32,1024]{1,0:T(8,128)S(1)} %get-tuple-element.46), channel_id=1, source_target_pairs={{0,8},{2,10},{4,12},{6,14},{8,16},{10,18},{12,20},{14,22},{16,24},... | collective-permute-start | bytes 393224 | tf_op jit(solution)/shard_map/ppermute | solution.py:260
  120.4 3.3 %collective-permute-start.26 = (f32[32,1024]{1,0:T(8,128)S(1)}, f32[32,1024]{1,0:T(8,128)S(1)}, u32[]{:S(2)}, u32[]{:S(2)}) collective-permute-start(f32[32,1024]{1,0:T(8,128)S(1)} %get-tuple-element.48), channel_id=1, source_target_pairs={{0,16},{2,18},{4,20},{6,22},{8,24},{10,26},{12,28},{14,30},{16,0},... | collective-permute-start | bytes 393224 | tf_op jit(solution)/shard_map/ppermute | solution.py:260
  123.6 4.6 %collective-permute-done.29 = f32[128,1024]{1,0:T(8,128)S(1)} collective-permute-done((f32[128,1024]{1,0:T(8,128)S(1)}, f32[128,1024]{1,0:T(8,128)S(1)}, u32[]{:S(2)}, u32[]{:S(2)}) %collective-permute-start.29) | collective-permute-done | bytes 524320 | tf_op jit(solution)/shard_map/ppermute | solution.py:255
  128.3 5.9 %collective-permute-start.27 = (f32[32,1024]{1,0:T(8,128)S(1)}, f32[32,1024]{1,0:T(8,128)S(1)}, u32[]{:S(2)}, u32[]{:S(2)}) collective-permute-start(f32[32,1024]{1,0:T(8,128)S(1)} %get-tuple-element.47), channel_id=1, source_target_pairs={{0,24},{2,26},{4,28},{6,30},{8,0},{10,2},{12,4},{14,6},{16,8},{18,... | collective-permute-start | bytes 393224 | tf_op jit(solution)/shard_map/ppermute | solution.py:260
  134.9 3.2 %collective-permute-done.27 = f32[32,1024]{1,0:T(8,128)S(1)} collective-permute-done((f32[32,1024]{1,0:T(8,128)S(1)}, f32[32,1024]{1,0:T(8,128)S(1)}, u32[]{:S(2)}, u32[]{:S(2)}) %collective-permute-start.27) | collective-permute-done | bytes 131104 | tf_op jit(solution)/shard_map/ppermute | solution.py:260
  138.1 4.3 %collective-permute-start.32 = (f32[32,1024]{1,0:T(8,128)S(1)}, f32[32,1024]{1,0:T(8,128)S(1)}, u32[]{:S(2)}, u32[]{:S(2)}) collective-permute-start(f32[32,1024]{1,0:T(8,128)S(1)} %get-tuple-element.50), channel_id=1, source_target_pairs={{0,24},{2,26},{4,28},{6,30},{8,0},{10,2},{12,4},{14,6},{16,8},{18,... | collective-permute-start | bytes 393224 | tf_op jit(solution)/shard_map/ppermute | solution.py:260
  142.6 3.3 %collective-permute-done.31 = f32[32,1024]{1,0:T(8,128)S(1)} collective-permute-done((f32[32,1024]{1,0:T(8,128)S(1)}, f32[32,1024]{1,0:T(8,128)S(1)}, u32[]{:S(2)}, u32[]{:S(2)}) %collective-permute-start.31) | collective-permute-done | bytes 131104 | tf_op jit(solution)/shard_map/ppermute | solution.py:260
  145.9 1.7 %collective-permute-start.10 = (f32[32,1024]{1,0:T(8,128)S(1)}, f32[32,1024]{1,0:T(8,128)S(1)}, u32[]{:S(2)}, u32[]{:S(2)}) collective-permute-start(f32[32,1024]{1,0:T(8,128)S(1)} %get-tuple-element.42), channel_id=1, source_target_pairs={{0,16},{2,18},{4,20},{6,22},{8,24},{10,26},{12,28},{14,30},{16,0},... | collective-permute-start | bytes 393224 | tf_op jit(solution)/shard_map/ppermute | solution.py:260
  147.7 3.4 %collective-permute-start.11 = (f32[32,1024]{1,0:T(8,128)S(1)}, f32[32,1024]{1,0:T(8,128)S(1)}, u32[]{:S(2)}, u32[]{:S(2)}) collective-permute-start(f32[32,1024]{1,0:T(8,128)S(1)} %get-tuple-element.41), channel_id=1, source_target_pairs={{0,24},{2,26},{4,28},{6,30},{8,0},{10,2},{12,4},{14,6},{16,8},{18,... | collective-permute-start | bytes 393224 | tf_op jit(solution)/shard_map/ppermute | solution.py:260
  151.1 2.3 %collective-permute-start.15 = (f32[32,1024]{1,0:T(8,128)S(1)}, f32[32,1024]{1,0:T(8,128)S(1)}, u32[]{:S(2)}, u32[]{:S(2)}) collective-permute-start(f32[32,1024]{1,0:T(8,128)S(1)} %get-tuple-element.43), channel_id=1, source_target_pairs={{0,8},{2,10},{4,12},{6,14},{8,16},{10,18},{12,20},{14,22},{16,24},... | collective-permute-start | bytes 393224 | tf_op jit(solution)/shard_map/ppermute | solution.py:260
  153.4 3.3 %collective-permute-start.16 = (f32[32,1024]{1,0:T(8,128)S(1)}, f32[32,1024]{1,0:T(8,128)S(1)}, u32[]{:S(2)}, u32[]{:S(2)}) collective-permute-start(f32[32,1024]{1,0:T(8,128)S(1)} %get-tuple-element.45), channel_id=1, source_target_pairs={{0,16},{2,18},{4,20},{6,22},{8,24},{10,26},{12,28},{14,30},{16,0},... | collective-permute-start | bytes 393224 | tf_op jit(solution)/shard_map/ppermute | solution.py:260
  156.8 3.4 %collective-permute-start.17 = (f32[32,1024]{1,0:T(8,128)S(1)}, f32[32,1024]{1,0:T(8,128)S(1)}, u32[]{:S(2)}, u32[]{:S(2)}) collective-permute-start(f32[32,1024]{1,0:T(8,128)S(1)} %get-tuple-element.44), channel_id=1, source_target_pairs={{0,24},{2,26},{4,28},{6,30},{8,0},{10,2},{12,4},{14,6},{16,8},{18,... | collective-permute-start | bytes 393224 | tf_op jit(solution)/shard_map/ppermute | solution.py:260
  161.1 2.7 %collective-permute-done.15 = f32[32,1024]{1,0:T(8,128)S(1)} collective-permute-done((f32[32,1024]{1,0:T(8,128)S(1)}, f32[32,1024]{1,0:T(8,128)S(1)}, u32[]{:S(2)}, u32[]{:S(2)}) %collective-permute-start.15) | collective-permute-done | bytes 131104 | tf_op jit(solution)/shard_map/ppermute | solution.py:260
  163.8 5.9 %collective-permute-done.16 = f32[32,1024]{1,0:T(8,128)S(1)} collective-permute-done((f32[32,1024]{1,0:T(8,128)S(1)}, f32[32,1024]{1,0:T(8,128)S(1)}, u32[]{:S(2)}, u32[]{:S(2)}) %collective-permute-start.16) | collective-permute-done | bytes 131104 | tf_op jit(solution)/shard_map/ppermute | solution.py:260
  (128 shorter events, 26.1 us)
Async XLA Ops:
  0.6 69.6 %copy-start = (bf16[32,32,512]{2,1,0:T(8,128)(2,1)S(1)}, bf16[32,32,512]{2,1,0:T(8,128)(2,1)}, u32[]{:S(2)}) copy-start(bf16[32,32,512]{2,1,0:T(8,128)(2,1)} %param.30) | copy-start | bytes 3145732
  0.6 19.8 %copy-start.23 = (bf16[2,32,512]{2,1,0:T(8,128)(2,1)S(1)}, bf16[2,32,512]{2,1,0:T(8,128)(2,1)}, u32[]{:S(2)}) copy-start(bf16[2,32,512]{2,1,0:T(8,128)(2,1)} %param.31) | copy-start | bytes 196612
  9.4 20.9 %collective-permute-start = (bf16[32,2176]{1,0:T(8,128)(2,1)}, bf16[32,2176]{1,0:T(8,128)(2,1)S(1)}, u32[]{:S(2)}, u32[]{:S(2)}) collective-permute-start(bf16[32,2176]{1,0:T(8,128)(2,1)} %get-tuple-element.16.refs_0_), channel_id=1, source_target_pairs={{0,24},{2,26},{4,28},{6,30},{8,0},{10,2},{12,4},{14,6},{16,8},{18,... | collective-permute-start | bytes 417800 | tf_op jit(solution)/shard_map/ppermute | solution.py:260
  14.4 16.4 %collective-permute-start.1 = (bf16[32,2176]{1,0:T(8,128)(2,1)}, bf16[32,2176]{1,0:T(8,128)(2,1)S(1)}, u32[]{:S(2)}, u32[]{:S(2)}) collective-permute-start(bf16[32,2176]{1,0:T(8,128)(2,1)} %get-tuple-element.16.refs_0_), channel_id=1, source_target_pairs={{0,16},{2,18},{4,20},{6,22},{8,24},{10,26},{12,28},{14,30},{16,0},... | collective-permute-start | bytes 417800 | tf_op jit(solution)/shard_map/ppermute | solution.py:260
  14.4 17.9 %collective-permute-start.2 = (bf16[32,2176]{1,0:T(8,128)(2,1)}, bf16[32,2176]{1,0:T(8,128)(2,1)S(1)}, u32[]{:S(2)}, u32[]{:S(2)}) collective-permute-start(bf16[32,2176]{1,0:T(8,128)(2,1)} %get-tuple-element.16.refs_0_), channel_id=1, source_target_pairs={{0,8},{2,10},{4,12},{6,14},{8,16},{10,18},{12,20},{14,22},{16,24},... | collective-permute-start | bytes 417800 | tf_op jit(solution)/shard_map/ppermute | solution.py:260
  15.5 8.2 %collective-permute-start.18 = (bf16[32,2176]{1,0:T(8,128)(2,1)}, bf16[32,2176]{1,0:T(8,128)(2,1)S(1)}, u32[]{:S(2)}, u32[]{:S(2)}) collective-permute-start(bf16[32,2176]{1,0:T(8,128)(2,1)} %get-tuple-element.23.refs_0_), channel_id=1, source_target_pairs={{0,4},{2,6},{4,0},{6,2},{8,12},{10,14},{12,8},{14,10},{16,20},{18,... | collective-permute-start | bytes 417800 | tf_op jit(solution)/shard_map/ppermute | solution.py:255
  17.0 54.4 %collective-permute-start.5 = (bf16[1024,384]{1,0:T(8,128)(2,1)}, bf16[1024,384]{1,0:T(8,128)(2,1)}, u32[]{:S(2)}, u32[]{:S(2)}) collective-permute-start(bf16[1024,384]{1,0:T(8,128)(2,1)} %bitcast.67), channel_id=1, source_target_pairs={{0,1},{1,0},{2,3},{3,2},{4,5},{5,4},{6,7},{7,6},{8,9},{9,8},{10,11... | collective-permute-start | bytes 2359304 | tf_op jit(solution)/shard_map/ppermute | solution.py:352
  23.7 28.4 %copy-start.13 = (f32[32,4,8]{2,1,0:T(4,128)}, f32[32,4,8]{2,1,0:T(4,128)S(1)}, u32[]{:S(2)}) copy-start(f32[32,4,8]{2,1,0:T(4,128)S(1)} %max.14) | copy-start | bytes 12292
  26.1 10.8 %copy-start.3 = (bf16[64,2176]{1,0:T(8,128)(2,1)S(1)}, bf16[64,2176]{1,0:T(8,128)(2,1)}, u32[]{:S(2)}) copy-start(bf16[64,2176]{1,0:T(8,128)(2,1)} %shard_map.181) | copy-start | bytes 835588
  26.1 10.8 %collective-permute-start.21 = (bf16[64,2176]{1,0:T(8,128)(2,1)}, bf16[64,2176]{1,0:T(8,128)(2,1)S(1)}, u32[]{:S(2)}, u32[]{:S(2)}) collective-permute-start(bf16[64,2176]{1,0:T(8,128)(2,1)} %shard_map.181), channel_id=1, source_target_pairs={{0,8},{2,10},{4,12},{6,14},{8,16},{10,18},{12,20},{14,22},{16,24},... | collective-permute-start | bytes 835592 | tf_op jit(solution)/shard_map/ppermute | solution.py:260
  30.3 3.0 %copy-start.16 = (bf16[32,2176]{1,0:T(8,128)(2,1)}, bf16[32,2176]{1,0:T(8,128)(2,1)S(1)}, u32[]{:S(2)}) copy-start(bf16[32,2176]{1,0:T(8,128)(2,1)S(1)} %collective-permute-done.refs_1_) | copy-start | bytes 417796
  30.3 41.2 %collective-permute-start.6 = (bf16[1024,384]{1,0:T(8,128)(2,1)}, bf16[1024,384]{1,0:T(8,128)(2,1)}, u32[]{:S(2)}, u32[]{:S(2)}) collective-permute-start(bf16[1024,384]{1,0:T(8,128)(2,1)} %bitcast.6.up_own_ref), channel_id=1, source_target_pairs={{0,1},{1,0},{2,3},{3,2},{4,5},{5,4},{6,7},{7,6},{8,9},{9,8},{10,11... | collective-permute-start | bytes 2359304 | tf_op jit(solution)/shard_map/ppermute | solution.py:352
  30.8 2.4 %copy-start.17 = (bf16[32,2176]{1,0:T(8,128)(2,1)}, bf16[32,2176]{1,0:T(8,128)(2,1)S(1)}, u32[]{:S(2)}) copy-start(bf16[32,2176]{1,0:T(8,128)(2,1)S(1)} %collective-permute-done.1.refs_2_) | copy-start | bytes 417796
  30.8 50.4 %collective-permute-start.12 = (bf16[384,1024]{1,0:T(8,128)(2,1)}, bf16[384,1024]{1,0:T(8,128)(2,1)}, u32[]{:S(2)}, u32[]{:S(2)}) collective-permute-start(bf16[384,1024]{1,0:T(8,128)(2,1)} %bitcast.7.down_ref), channel_id=1, source_target_pairs={{0,1},{1,0},{2,3},{3,2},{4,5},{5,4},{6,7},{7,6},{8,9},{9,8},{10,11... | collective-permute-start | bytes 2359304 | tf_op jit(solution)/shard_map/ppermute | solution.py:352
  32.3 14.8 %collective-permute-start.20 = (bf16[64,2176]{1,0:T(8,128)(2,1)}, bf16[64,2176]{1,0:T(8,128)(2,1)S(1)}, u32[]{:S(2)}, u32[]{:S(2)}) collective-permute-start(bf16[64,2176]{1,0:T(8,128)(2,1)} %shard_map.181), channel_id=1, source_target_pairs={{0,16},{2,18},{4,20},{6,22},{8,24},{10,26},{12,28},{14,30},{16,0},... | collective-permute-start | bytes 835592 | tf_op jit(solution)/shard_map/ppermute | solution.py:260
  36.8 12.0 %collective-permute-start.19 = (bf16[64,2176]{1,0:T(8,128)(2,1)S(1)}, bf16[64,2176]{1,0:T(8,128)(2,1)S(1)}, u32[]{:S(2)}, u32[]{:S(2)}) collective-permute-start(bf16[64,2176]{1,0:T(8,128)(2,1)S(1)} %copy-done.3), channel_id=1, source_target_pairs={{0,24},{2,26},{4,28},{6,30},{8,0},{10,2},{12,4},{14,6},{16,8},{18,... | collective-permute-start | bytes 835592 | tf_op jit(solution)/shard_map/ppermute | solution.py:260
  47.1 14.8 %collective-permute-start.3 = (bf16[128,2176]{1,0:T(8,128)(2,1)}, bf16[128,2176]{1,0:T(8,128)(2,1)}, u32[]{:S(2)}, u32[]{:S(2)}) collective-permute-start(bf16[128,2176]{1,0:T(8,128)(2,1)} %shard_map.177.refs_0_), channel_id=1, source_target_pairs={{0,4},{2,6},{4,0},{6,2},{8,12},{10,14},{12,8},{14,10},{16,20},{18,... | collective-permute-start | bytes 1671176 | tf_op jit(solution)/shard_map/ppermute | solution.py:255
  49.5 2.5 %copy-start.9 = (bf16[32,32,512]{2,1,0:T(8,128)(2,1)S(1)}, bf16[32,32,512]{2,1,0:T(8,128)(2,1)}, u32[]{:S(2)}) copy-start(bf16[32,32,512]{2,1,0:T(8,128)(2,1)} %param.29) | copy-start | bytes 3145732
  52.0 19.4 %collective-permute-start.22 = (bf16[256,2176]{1,0:T(8,128)(2,1)}, bf16[256,2176]{1,0:T(8,128)(2,1)S(1)}, u32[]{:S(2)}, u32[]{:S(2)}) collective-permute-start(bf16[256,2176]{1,0:T(8,128)(2,1)} %shard_map.182.here_ref), channel_id=1, source_target_pairs={{0,2},{2,0},{4,6},{6,4},{8,10},{10,8},{12,14},{14,12},{16,18},{18,... | collective-permute-start | bytes 3342344 | tf_op jit(solution)/shard_map/ppermute | solution.py:255
  64.3 2.2 %copy-start.14 = (f32[32,4,8]{2,1,0:T(4,128)S(1)}, f32[32,4,8]{2,1,0:T(4,128)}, u32[]{:S(2)}) copy-start(f32[32,4,8]{2,1,0:T(4,128)} %copy-done.13) | copy-start | bytes 12292
  64.3 2.2 %copy-start.20 = (f32[32,4,8,2]{2,3,1,0:T(2,128)S(1)}, f32[32,4,8,2]{2,3,1,0:T(2,128)}, u32[]{:S(2)}) copy-start(f32[32,4,8,2]{2,3,1,0:T(2,128)} %get-tuple-element.67) | copy-start | bytes 24580
  64.3 21.5 %collective-permute-start.4 = (bf16[256,2176]{1,0:T(8,128)(2,1)}, bf16[256,2176]{1,0:T(8,128)(2,1)S(1)}, u32[]{:S(2)}, u32[]{:S(2)}) collective-permute-start(bf16[256,2176]{1,0:T(8,128)(2,1)} %shard_map.178.here_ref), channel_id=1, source_target_pairs={{0,2},{2,0},{4,6},{6,4},{8,10},{10,8},{12,14},{14,12},{16,18},{18,... | collective-permute-start | bytes 3342344 | tf_op jit(solution)/shard_map/ppermute | solution.py:255
  67.9 2.3 %copy-start.25 = (bf16[2,32,4,128]{3,2,1,0:T(4,128)(2,1)}, bf16[2,32,4,128]{3,2,1,0:T(4,128)(2,1)S(1)}, u32[]{:S(2)}) copy-start(bf16[2,32,4,128]{3,2,1,0:T(4,128)(2,1)S(1)} %reshape.92) | copy-start | bytes 196612
  79.3 22.7 %collective-permute-start.23 = (f32[256,1024]{1,0:T(8,128)}, f32[256,1024]{1,0:T(8,128)S(1)}, u32[]{:S(2)}, u32[]{:S(2)}) collective-permute-start(f32[256,1024]{1,0:T(8,128)} %get-tuple-element.25), channel_id=1, source_target_pairs={{0,2},{2,0},{4,6},{6,4},{8,10},{10,8},{12,14},{14,12},{16,18},{18,... | collective-permute-start | bytes 3145736 | tf_op jit(solution)/shard_map/ppermute | solution.py:255
  81.2 3.3 %copy-start.22 = (f32[32,4,8,2]{2,3,1,0:T(2,128)S(1)}, f32[32,4,8,2]{2,3,1,0:T(2,128)}, u32[]{:S(2)}) copy-start(f32[32,4,8,2]{2,3,1,0:T(2,128)} %copy-done.21) | copy-start | bytes 24580
  81.2 3.3 %copy-start.26 = (bf16[2,32,4,128]{3,2,1,0:T(4,128)(2,1)S(1)}, bf16[2,32,4,128]{3,2,1,0:T(4,128)(2,1)}, u32[]{:S(2)}) copy-start(bf16[2,32,4,128]{3,2,1,0:T(4,128)(2,1)} %copy-done.25) | copy-start | bytes 196612
  84.5 18.2 %collective-permute-start.28 = (f32[256,1024]{1,0:T(8,128)}, f32[256,1024]{1,0:T(8,128)}, u32[]{:S(2)}, u32[]{:S(2)}) collective-permute-start(f32[256,1024]{1,0:T(8,128)} %get-tuple-element.29), channel_id=1, source_target_pairs={{0,2},{2,0},{4,6},{6,4},{8,10},{10,8},{12,14},{14,12},{16,18},{18,... | collective-permute-start | bytes 3145736 | tf_op jit(solution)/shard_map/ppermute | solution.py:255
  93.7 12.1 %collective-permute-start.7 = (f32[256,1024]{1,0:T(8,128)}, f32[256,1024]{1,0:T(8,128)}, u32[]{:S(2)}, u32[]{:S(2)}) collective-permute-start(f32[256,1024]{1,0:T(8,128)} %get-tuple-element.18), channel_id=1, source_target_pairs={{0,2},{2,0},{4,6},{6,4},{8,10},{10,8},{12,14},{14,12},{16,18},{18,... | collective-permute-start | bytes 3145736 | tf_op jit(solution)/shard_map/ppermute | solution.py:255
  100.0 8.2 %collective-permute-start.13 = (f32[256,1024]{1,0:T(8,128)}, f32[256,1024]{1,0:T(8,128)}, u32[]{:S(2)}, u32[]{:S(2)}) collective-permute-start(f32[256,1024]{1,0:T(8,128)} %get-tuple-element.22), channel_id=1, source_target_pairs={{0,2},{2,0},{4,6},{6,4},{8,10},{10,8},{12,14},{14,12},{16,18},{18,... | collective-permute-start | bytes 3145736 | tf_op jit(solution)/shard_map/ppermute | solution.py:255
  102.2 14.9 %collective-permute-start.24 = (f32[128,1024]{1,0:T(8,128)S(1)}, f32[128,1024]{1,0:T(8,128)S(1)}, u32[]{:S(2)}, u32[]{:S(2)}) collective-permute-start(f32[128,1024]{1,0:T(8,128)S(1)} %get-tuple-element.37), channel_id=1, source_target_pairs={{0,4},{2,6},{4,0},{6,2},{8,12},{10,14},{12,8},{14,10},{16,20},{18,... | collective-permute-start | bytes 1572872 | tf_op jit(solution)/shard_map/ppermute | solution.py:255
  103.2 2.6 %copy-start.6 = (f32[256,1024]{1,0:T(8,128)S(1)}, f32[256,1024]{1,0:T(8,128)}, u32[]{:S(2)}) copy-start(f32[256,1024]{1,0:T(8,128)} %get-tuple-element.17) | copy-start | bytes 3145732
  104.6 23.6 %collective-permute-start.29 = (f32[128,1024]{1,0:T(8,128)S(1)}, f32[128,1024]{1,0:T(8,128)S(1)}, u32[]{:S(2)}, u32[]{:S(2)}) collective-permute-start(f32[128,1024]{1,0:T(8,128)S(1)} %get-tuple-element.39), channel_id=1, source_target_pairs={{0,4},{2,6},{4,0},{6,2},{8,12},{10,14},{12,8},{14,10},{16,20},{18,... | collective-permute-start | bytes 1572872 | tf_op jit(solution)/shard_map/ppermute | solution.py:255
  105.8 2.5 %copy-start.7 = (f32[256,1024]{1,0:T(8,128)S(1)}, f32[256,1024]{1,0:T(8,128)}, u32[]{:S(2)}) copy-start(f32[256,1024]{1,0:T(8,128)} %get-tuple-element.21) | copy-start | bytes 3145732
  107.2 38.6 %collective-permute-start.8 = (f32[128,1024]{1,0:T(8,128)S(1)}, f32[128,1024]{1,0:T(8,128)S(1)}, u32[]{:S(2)}, u32[]{:S(2)}) collective-permute-start(f32[128,1024]{1,0:T(8,128)S(1)} %get-tuple-element.33), channel_id=1, source_target_pairs={{0,4},{2,6},{4,0},{6,2},{8,12},{10,14},{12,8},{14,10},{16,20},{18,... | collective-permute-start | bytes 1572872 | tf_op jit(solution)/shard_map/ppermute | solution.py:255
  109.6 41.5 %collective-permute-start.14 = (f32[128,1024]{1,0:T(8,128)S(1)}, f32[128,1024]{1,0:T(8,128)S(1)}, u32[]{:S(2)}, u32[]{:S(2)}) collective-permute-start(f32[128,1024]{1,0:T(8,128)S(1)} %get-tuple-element.35), channel_id=1, source_target_pairs={{0,4},{2,6},{4,0},{6,2},{8,12},{10,14},{12,8},{14,10},{16,20},{18,... | collective-permute-start | bytes 1572872 | tf_op jit(solution)/shard_map/ppermute | solution.py:255
  117.1 17.2 %collective-permute-start.25 = (f32[32,1024]{1,0:T(8,128)S(1)}, f32[32,1024]{1,0:T(8,128)S(1)}, u32[]{:S(2)}, u32[]{:S(2)}) collective-permute-start(f32[32,1024]{1,0:T(8,128)S(1)} %get-tuple-element.46), channel_id=1, source_target_pairs={{0,8},{2,10},{4,12},{6,14},{8,16},{10,18},{12,20},{14,22},{16,24},... | collective-permute-start | bytes 393224 | tf_op jit(solution)/shard_map/ppermute | solution.py:260
  120.4 14.0 %collective-permute-start.26 = (f32[32,1024]{1,0:T(8,128)S(1)}, f32[32,1024]{1,0:T(8,128)S(1)}, u32[]{:S(2)}, u32[]{:S(2)}) collective-permute-start(f32[32,1024]{1,0:T(8,128)S(1)} %get-tuple-element.48), channel_id=1, source_target_pairs={{0,16},{2,18},{4,20},{6,22},{8,24},{10,26},{12,28},{14,30},{16,0},... | collective-permute-start | bytes 393224 | tf_op jit(solution)/shard_map/ppermute | solution.py:260
  128.3 9.9 %collective-permute-start.27 = (f32[32,1024]{1,0:T(8,128)S(1)}, f32[32,1024]{1,0:T(8,128)S(1)}, u32[]{:S(2)}, u32[]{:S(2)}) collective-permute-start(f32[32,1024]{1,0:T(8,128)S(1)} %get-tuple-element.47), channel_id=1, source_target_pairs={{0,24},{2,26},{4,28},{6,30},{8,0},{10,2},{12,4},{14,6},{16,8},{18,... | collective-permute-start | bytes 393224 | tf_op jit(solution)/shard_map/ppermute | solution.py:260
  134.3 8.3 %collective-permute-start.30 = (f32[32,1024]{1,0:T(8,128)S(1)}, f32[32,1024]{1,0:T(8,128)S(1)}, u32[]{:S(2)}, u32[]{:S(2)}) collective-permute-start(f32[32,1024]{1,0:T(8,128)S(1)} %get-tuple-element.49), channel_id=1, source_target_pairs={{0,8},{2,10},{4,12},{6,14},{8,16},{10,18},{12,20},{14,22},{16,24},... | collective-permute-start | bytes 393224 | tf_op jit(solution)/shard_map/ppermute | solution.py:260
  134.3 11.5 %collective-permute-start.31 = (f32[32,1024]{1,0:T(8,128)S(1)}, f32[32,1024]{1,0:T(8,128)S(1)}, u32[]{:S(2)}, u32[]{:S(2)}) collective-permute-start(f32[32,1024]{1,0:T(8,128)S(1)} %get-tuple-element.51), channel_id=1, source_target_pairs={{0,16},{2,18},{4,20},{6,22},{8,24},{10,26},{12,28},{14,30},{16,0},... | collective-permute-start | bytes 393224 | tf_op jit(solution)/shard_map/ppermute | solution.py:260
  138.1 7.7 %collective-permute-start.32 = (f32[32,1024]{1,0:T(8,128)S(1)}, f32[32,1024]{1,0:T(8,128)S(1)}, u32[]{:S(2)}, u32[]{:S(2)}) collective-permute-start(f32[32,1024]{1,0:T(8,128)S(1)} %get-tuple-element.50), channel_id=1, source_target_pairs={{0,24},{2,26},{4,28},{6,30},{8,0},{10,2},{12,4},{14,6},{16,8},{18,... | collective-permute-start | bytes 393224 | tf_op jit(solution)/shard_map/ppermute | solution.py:260
  145.9 10.9 %collective-permute-start.10 = (f32[32,1024]{1,0:T(8,128)S(1)}, f32[32,1024]{1,0:T(8,128)S(1)}, u32[]{:S(2)}, u32[]{:S(2)}) collective-permute-start(f32[32,1024]{1,0:T(8,128)S(1)} %get-tuple-element.42), channel_id=1, source_target_pairs={{0,16},{2,18},{4,20},{6,22},{8,24},{10,26},{12,28},{14,30},{16,0},... | collective-permute-start | bytes 393224 | tf_op jit(solution)/shard_map/ppermute | solution.py:260
  147.7 12.5 %collective-permute-start.11 = (f32[32,1024]{1,0:T(8,128)S(1)}, f32[32,1024]{1,0:T(8,128)S(1)}, u32[]{:S(2)}, u32[]{:S(2)}) collective-permute-start(f32[32,1024]{1,0:T(8,128)S(1)} %get-tuple-element.41), channel_id=1, source_target_pairs={{0,24},{2,26},{4,28},{6,30},{8,0},{10,2},{12,4},{14,6},{16,8},{18,... | collective-permute-start | bytes 393224 | tf_op jit(solution)/shard_map/ppermute | solution.py:260
  151.0 10.0 %collective-permute-start.9 = (f32[32,1024]{1,0:T(8,128)S(1)}, f32[32,1024]{1,0:T(8,128)S(1)}, u32[]{:S(2)}, u32[]{:S(2)}) collective-permute-start(f32[32,1024]{1,0:T(8,128)S(1)} %get-tuple-element.40), channel_id=1, source_target_pairs={{0,8},{2,10},{4,12},{6,14},{8,16},{10,18},{12,20},{14,22},{16,24},... | collective-permute-start | bytes 393224 | tf_op jit(solution)/shard_map/ppermute | solution.py:260
  151.0 18.7 %copy-start.10 = (bf16[2,32,2048]{2,1,0:T(8,128)(2,1)S(1)}, bf16[2,32,2048]{2,1,0:T(8,128)(2,1)}, u32[]{:S(2)}) copy-start(bf16[2,32,2048]{2,1,0:T(8,128)(2,1)} %hidden_ref.1) | copy-start | bytes 786436
  151.1 12.7 %collective-permute-start.15 = (f32[32,1024]{1,0:T(8,128)S(1)}, f32[32,1024]{1,0:T(8,128)S(1)}, u32[]{:S(2)}, u32[]{:S(2)}) collective-permute-start(f32[32,1024]{1,0:T(8,128)S(1)} %get-tuple-element.43), channel_id=1, source_target_pairs={{0,8},{2,10},{4,12},{6,14},{8,16},{10,18},{12,20},{14,22},{16,24},... | collective-permute-start | bytes 393224 | tf_op jit(solution)/shard_map/ppermute | solution.py:260
  153.4 16.3 %collective-permute-start.16 = (f32[32,1024]{1,0:T(8,128)S(1)}, f32[32,1024]{1,0:T(8,128)S(1)}, u32[]{:S(2)}, u32[]{:S(2)}) collective-permute-start(f32[32,1024]{1,0:T(8,128)S(1)} %get-tuple-element.45), channel_id=1, source_target_pairs={{0,16},{2,18},{4,20},{6,22},{8,24},{10,26},{12,28},{14,30},{16,0},... | collective-permute-start | bytes 393224 | tf_op jit(solution)/shard_map/ppermute | solution.py:260
  156.8 12.9 %collective-permute-start.17 = (f32[32,1024]{1,0:T(8,128)S(1)}, f32[32,1024]{1,0:T(8,128)S(1)}, u32[]{:S(2)}, u32[]{:S(2)}) collective-permute-start(f32[32,1024]{1,0:T(8,128)S(1)} %get-tuple-element.44), channel_id=1, source_target_pairs={{0,24},{2,26},{4,28},{6,30},{8,0},{10,2},{12,4},{14,6},{16,8},{18,... | collective-permute-start | bytes 393224 | tf_op jit(solution)/shard_map/ppermute | solution.py:260
  (12 other events, 16.2 us)
